TPU v7x, 512 devices: a whole 4x8x8 slice. The times are simulated.
512 devices in a mesh: stat: 16 (over z, core), tile: 32 (over x, y).
Axes of the slice: x: 4, y: 8, z: 8, core: 2. Of those that a mesh axis runs over, the one named last changes fastest.
Arguments:
- visibilities: float32 [16384, 8, 256], P(('stat', 'tile')), may hold values from -6 to 6
- weights: float32 [16384, 256], P(('stat', 'tile')), may hold values from 0.2 to 2
- uv_coords: float32 [16384, 2, 16], P(('stat', 'tile')), may hold values from -8 to 8
- freq_ratio: float32 [16], replicated, may hold values from 0.8 to 1.25
- screens: bfloat16 [512, 2, 1024], P('stat'), may hold values from -6 to 6
- stations: int32 [16384, 2], P(('stat', 'tile')), may hold values from 0 to 511
- offsets: int32 [16384, 2], P(('stat', 'tile')), may hold values from 0 to 224
- tile_ids: int32 [16384, 1], P(('stat', 'tile')), may hold values from 0 to 31; in each aligned block of 32 rows (0 to 31, 32 to 63, ...) at most 2 rows name the same one
Outputs:
- uv_grid: float32 [32, 8, 256, 256], P('tile', None, 'stat')
Inputs may be any that keep to these rules, and one draw needn't show every extreme that they name: `tile_ids`: among the 32 rows of one device at most 2 name the same tile, and in every draw some device has exactly 2 rows naming one tile.
All inputs are finite; a program needn't handle non-finite values.
Results may differ from a plain program's by a relative error of at most 0.012.
Values may be sent and summed in bfloat16 or wider, within the bound.
No kernel may reach another device: no remote copies, remote signals or barrier semaphores. Data moves between devices by JAX's collectives and lax.ppermute only.
A program may use at most 64 MiB of HBM per device.

v0:
```python
import functools
import math

import jax
import jax.numpy as jnp
import numpy as np
from jax import lax
from jax.experimental import pallas as pl
from jax.experimental.pallas import tpu as pltpu
from jax.sharding import PartitionSpec as P

SUB = 32
TS = 256
K = 256
SLOTS = 64
PEERS = 32
F32 = jnp.float32
BF16 = jnp.bfloat16

ROW_L = np.array([4 * (r % 8) + r // 8 for r in range(SUB)])
LANE = np.arange(256)
LANE_I = LANE % 16
LANE_P = (LANE // 16) % 4
LANE_RI = (LANE // 64) % 2
LANE_M = np.where(LANE < 128, 16 + LANE_I, 15 - LANE_I)


def spread_tables():
    out = np.zeros((4, 256, 256), np.float32)
    for part in range(3):
        for t in range(16):
            out[0, part * 32 + t, t * 16 : (t + 1) * 16] = 1.0
            out[1, part * 32 + 16 + t, t * 16 : (t + 1) * 16] = 1.0
    out[2, 101, :] = 1.0
    out[3, 103, :] = 1.0
    return out


def replicate_tables():
    cell = np.arange(128) % 32
    rep = (cell[:, None] == LANE_M[None, :]).astype(np.float32)
    sign = np.where(LANE_RI == 0, -1.0, 1.0).astype(np.float32)
    return np.stack([rep, rep * sign[None, :]])


def column_table():
    n = np.arange(256)
    ri, p, v = n // 128, (n // 32) % 4, n % 32
    angle = -2.0 * np.pi / SUB * (LANE_M[:, None] - 16.0) * (v[None, :] - 16.0)
    cos, sin = np.cos(angle), np.sin(angle)
    same = LANE_RI[:, None] == ri[None, :]
    val = np.where(same, cos, np.where(LANE_RI[:, None] == 1, -sin, sin))
    return np.where(LANE_P[:, None] == p[None, :], val, 0.0)


def row_table():
    out_ri, u = np.arange(64) // 32, np.arange(64) % 32
    in_ri, l = np.arange(64) // 32, ROW_L[np.arange(64) % 32]
    angle = -2.0 * np.pi / SUB * (u[:, None] - 16.0) * (l[None, :] - 16.0)
    cos, sin = np.cos(angle), np.sin(angle)
    same = out_ri[:, None] == in_ri[None, :]
    return np.where(same, cos, np.where(in_ri[None, :] == 1, -sin, sin))


def taper_table():
    flat = np.arange(1024)
    l, m = flat // 32, flat % 32
    one = np.sin(np.pi * (np.arange(SUB) + 0.5) / SUB)
    return (one[l] * one[m] / (K * SUB)).reshape(8, 128).astype(np.float32)


def fit_turns():
    s = (0.5 * np.cos(np.pi * (np.arange(400) + 0.5) / 800)) ** 2
    r = np.sqrt(s)
    cheb = np.polynomial.chebyshev.Chebyshev.fit
    cos = cheb(s, np.cos(2 * np.pi * r), 7, domain=[0, 0.25]).convert(kind=np.polynomial.Polynomial)
    sin = cheb(s, np.sin(2 * np.pi * r) / r, 6, domain=[0, 0.25]).convert(kind=np.polynomial.Polynomial)
    return [float(c) for c in cos.coef], [float(c) for c in sin.coef]


COS_C, SIN_C = fit_turns()


def horner(coef, s):
    acc = jnp.full_like(s, coef[-1])
    for c in coef[-2::-1]:
        acc = acc * s + c
    return acc


def cos_sin_turns(turns):
    r = turns - jnp.round(turns)
    s = r * r
    return horner(COS_C, s), horner(SIN_C, s) * r


def pack_kernel(tile_ref, vis_ref, weight_ref, meta_ref, out_ref, src_ref, count_ref):
    def clear(i, c):
        src_ref[2 * i] = -1
        src_ref[2 * i + 1] = -1
        count_ref[i] = 0
        return c

    lax.fori_loop(0, PEERS, clear, 0, unroll=8)

    def assign(s, c):
        t = tile_ref[s]
        before = count_ref[t]
        src_ref[2 * t + before] = s
        count_ref[t] = before + 1
        return c

    lax.fori_loop(0, 32, assign, 0, unroll=4)
    row = lax.broadcasted_iota(jnp.int32, (8, 256), 0)

    def one_peer(n, c):
        blocks = []
        meta = jnp.zeros((8, 256), F32)
        for j in range(2):
            s = src_ref[2 * n + j]
            valid = s >= 0
            at = jnp.maximum(s, 0)
            weighted = vis_ref[at] * weight_ref[pl.ds(at, 1), :]
            blocks.append(jnp.where(valid, weighted, 0.0))
            meta = jnp.where(jnp.logical_and(row == j, valid), meta_ref[pl.ds(at, 1), :], meta)
        blocks.append(meta)
        out_ref[n] = jnp.concatenate(blocks, axis=0).astype(BF16)
        return c

    lax.fori_loop(0, PEERS, one_peer, 0, unroll=4)


def image_kernel(recv_ref, freq_ref, spread_ref, xrow_ref, ycol_ref, i_ref, j_ref, meta_ref, du_ref, dv_ref):
    for n in range(PEERS):
        meta_ref[n] = recv_ref[n, 16:24, :].astype(F32)
    meta = meta_ref[...].reshape(256, 256).astype(BF16)
    freq = freq_ref[...]

    def spread(k):
        return jnp.dot(meta, spread_ref[k], preferred_element_type=F32)

    du_ref[...] = (spread(0) * freq + spread(2)).reshape(PEERS, 8, 256)
    dv_ref[...] = (spread(1) * freq + spread(3)).reshape(PEERS, 8, 256)
    lane = lax.broadcasted_iota(jnp.int32, (SUB, 128), 1)
    sign = jnp.where(lane < 64, -1.0, 1.0).astype(F32)

    def one_peer(n, c):
        for j in range(2):
            du = du_ref[n, j : j + 1, :]
            dv = dv_ref[n, j : j + 1, :]
            cu, su = cos_sin_turns(xrow_ref[...] * du - dv * (0.5 / SUB))
            cv, sv = cos_sin_turns(ycol_ref[...] * dv)
            left = jnp.concatenate([cu.astype(BF16), su.astype(BF16)], axis=0)
            w = recv_ref[n, 8 * j : 8 * j + 8, :].astype(F32)
            nsv = -sv
            rows = [(w[q : q + 1, :] * cv).astype(BF16) for q in range(8)]
            rows += [(w[q + 4 : q + 5, :] * nsv).astype(BF16) for q in range(4)]
            rows += [(w[q : q + 1, :] * sv).astype(BF16) for q in range(4)]
            right = jnp.concatenate(rows, axis=0)
            prod = lax.dot_general(left, right, (((1,), (1,)), ((), ())), preferred_element_type=F32)
            cc, cs = prod[:32, :128], prod[:32, 128:]
            sc, ss = prod[32:, :128], prod[32:, 128:]
            slot = 2 * n + j
            for half, (a, b) in enumerate(((cc + cs, sc + ss), (cc - cs, sc - ss))):
                image = a + sign * pltpu.roll(b, 64, 1)
                i_ref[slot, :, 128 * half : 128 * half + 128] = image
                j_ref[slot, :, 128 * half : 128 * half + 128] = pltpu.roll(image, 64, 1)
        return c

    lax.fori_loop(0, PEERS, one_peer, 0)


GROUP = 4


def grid_kernel(ints_ref, i_ref, j_ref, screen_ref, taper_ref, rep_ref, col_ref, row_ref, out_ref, acc_ref):
    acc_ref[...] = jnp.zeros(acc_ref.shape, F32)
    taper = taper_ref[...]
    lane = lax.broadcasted_iota(jnp.int32, (8, 128), 1)
    sub = lax.broadcasted_iota(jnp.int32, (8, 128), 0)
    cell = lane % 32
    group_mask = [lane // 32 == a for a in range(4)]

    def one_group(g, c):
        lhs_re, lhs_im = [], []
        for k in range(GROUP):
            base = (g * GROUP + k) * 8
            sp = screen_ref[ints_ref[base] * 32 + ints_ref[base + 1]].astype(F32)
            sq = screen_ref[ints_ref[base + 2] * 32 + ints_ref[base + 3]].astype(F32)
            pr, pi, qr, qi = sp[:8], sp[8:], sq[:8], sq[8:]
            gain_re = (pr * qr + pi * qi) * taper
            gain_im = (pr * qi - pi * qr) * taper
            lhs_re += [jnp.where(m, gain_re, 0.0) for m in group_mask]
            lhs_im += [jnp.where(m, gain_im, 0.0) for m in group_mask]
        wide_re = jnp.dot(jnp.concatenate(lhs_re, 0).astype(BF16), rep_ref[0], preferred_element_type=F32)
        wide_im = jnp.dot(jnp.concatenate(lhs_im, 0).astype(BF16), rep_ref[1], preferred_element_type=F32)
        image = i_ref[pl.ds(g * GROUP, GROUP)].reshape(GROUP * SUB, 256)
        swapped = j_ref[pl.ds(g * GROUP, GROUP)].reshape(GROUP * SUB, 256)
        corrected = (wide_re * image + wide_im * swapped).astype(BF16)
        half = jnp.dot(corrected, col_ref[...], preferred_element_type=F32).astype(BF16)
        stacked = jnp.concatenate(
            [
                jnp.concatenate([half[k * 32 : k * 32 + 32, :128], half[k * 32 : k * 32 + 32, 128:]], axis=0)
                for k in range(GROUP)
            ],
            axis=1,
        )
        cells = jnp.dot(row_ref[...], stacked, preferred_element_type=F32)
        for k in range(GROUP):
            base = (g * GROUP + k) * 8
            row8, row_shift = ints_ref[base + 4], ints_ref[base + 5]
            col32, col_shift = ints_ref[base + 6], ints_ref[base + 7]
            keep_col = cell >= col_shift
            keep_row = sub >= row_shift
            for ri in range(2):
                for part in range(4):
                    s = cells[ri * 32 + part * 8 : ri * 32 + part * 8 + 8, k * 128 : k * 128 + 128]
                    near = jnp.where(keep_col, s, 0.0)
                    far = s - near
                    for piece, at in ((near, col32), (far, col32 + 1)):
                        if part == 0:
                            top = jnp.where(keep_row, piece, 0.0)
                            acc_ref[ri, at, row8] += top
                            acc_ref[ri, at, row8 + 4] += piece - top
                        else:
                            acc_ref[ri, at, row8 + part] += piece
        return c

    lax.fori_loop(0, SLOTS // GROUP, one_group, 0)
    for band in range(16):
        for ri in range(2):
            for a in range(8):
                piece = acc_ref[ri, a, 2 * band : 2 * band + 2].reshape(16, 128)
                out_ref[band, (ri * 8 + a) * 16 : (ri * 8 + a) * 16 + 16, :] = piece.astype(BF16)


def sum_kernel(in_ref, out_ref):
    lane = lax.broadcasted_iota(jnp.int32, (16, 128), 1) // 32
    masks = [lane == a for a in range(4)]
    for ri in range(2):
        for h in range(2):
            parts = []
            for a in range(4):
                at = (ri * 8 + h * 4 + a) * 16
                total = in_ref[0, at : at + 16, :].astype(F32)
                for s in range(1, 16):
                    total = total + in_ref[s, at : at + 16, :].astype(F32)
                parts.append(total)
            for p in range(4):
                row = jnp.zeros((16, 128), F32)
                for a in range(4):
                    shift = (32 * (a - p)) % 128
                    moved = pltpu.roll(parts[a], shift, 1) if shift else parts[a]
                    row = jnp.where(masks[a], moved, row)
                out_ref[0, ri * 4 + p, :, 128 * h : 128 * h + 128] = row


VM = pl.BlockSpec(memory_space=pltpu.VMEM)
SM = pl.BlockSpec(memory_space=pltpu.SMEM)
call = functools.partial(
    pl.pallas_call, compiler_params=pltpu.CompilerParams(vmem_limit_bytes=48 << 20)
)


def pack(tile_of, visibilities, weights, meta):
    return call(
        pack_kernel,
        out_shape=jax.ShapeDtypeStruct((PEERS, 24, 256), BF16),
        in_specs=[SM, VM, VM, VM],
        out_specs=VM,
        scratch_shapes=[pltpu.SMEM((SLOTS,), jnp.int32), pltpu.SMEM((PEERS,), jnp.int32)],
        name="pack",
    )(tile_of, visibilities, weights, meta)


def images(recv, freq_row):
    xrow = np.broadcast_to(((ROW_L - 16.0) / SUB)[:, None], (SUB, 256)).astype(np.float32)
    ycol = np.broadcast_to(((np.arange(16) + 0.5) / SUB)[:, None], (16, 256)).astype(np.float32)
    shape = jax.ShapeDtypeStruct((SLOTS, SUB, 256), F32)
    return call(
        image_kernel,
        out_shape=(shape, shape),
        in_specs=[VM] * 5,
        out_specs=(VM, VM),
        scratch_shapes=[pltpu.VMEM((PEERS, 8, 256), F32)] * 3,
        name="images",
    )(recv, freq_row, jnp.asarray(spread_tables(), BF16), jnp.asarray(xrow), jnp.asarray(ycol))


def grid_tile(ints, image, swapped, screens):
    return call(
        grid_kernel,
        out_shape=jax.ShapeDtypeStruct((16, 256, 128), BF16),
        in_specs=[SM] + [VM] * 7,
        out_specs=VM,
        scratch_shapes=[pltpu.VMEM((2, 9, 33, 8, 128), F32)],
        name="grid_tile",
    )(
        ints,
        image,
        swapped,
        screens,
        jnp.asarray(taper_table()),
        jnp.asarray(replicate_tables(), BF16),
        jnp.asarray(column_table(), BF16),
        jnp.asarray(row_table(), BF16),
    )


def band_sum(arrived):
    return call(
        sum_kernel,
        out_shape=jax.ShapeDtypeStruct((1, 8, 16, 256), F32),
        in_specs=[VM],
        out_specs=VM,
        name="band_sum",
    )(arrived)


def make_meta(uv_coords, stations, offsets):
    uv = uv_coords.reshape(32, 32)
    hi = lax.reduce_precision(uv, 8, 7)
    mid = lax.reduce_precision(uv - hi, 8, 7)
    low = (uv - hi) - mid
    p, q = stations[:, 0:1], stations[:, 1:2]
    r, c = offsets[:, 0:1], offsets[:, 1:2]
    ints = [p // 32, p % 32, q // 32, q % 32, r // 8, r % 8, c // 32, c % 32]
    return jnp.concatenate(
        [hi, mid, low] + [i.astype(F32) for i in ints] + [jnp.zeros((32, 152), F32)], axis=1
    )


def on_device(visibilities, weights, uv_coords, freq_ratio, screens, stations, offsets, tile_ids):
    everyone = lax.all_gather(screens.reshape(32, 16, 128), "stat", axis=0, tiled=True)
    meta = make_meta(uv_coords, stations, offsets)
    packed = pack(tile_ids[:, 0], visibilities, weights, meta)
    recv = lax.all_to_all(packed, "tile", split_axis=0, concat_axis=0, tiled=True)
    ints = recv[:, 16:18, 96:104].astype(jnp.int32).reshape(SLOTS * 8)
    image, swapped = images(recv, jnp.tile(freq_ratio, 16)[None, :])
    partial = grid_tile(ints, image, swapped, everyone)
    arrived = lax.all_to_all(partial, "stat", split_axis=0, concat_axis=0, tiled=True)
    return band_sum(arrived)


def solution(mesh):
    placed = (
        P(("stat", "tile"), None, None),
        P(("stat", "tile"), None),
        P(("stat", "tile"), None, None),
        P(),
        P("stat", None, None),
        P(("stat", "tile"), None),
        P(("stat", "tile"), None),
        P(("stat", "tile"), None),
    )
    return jax.shard_map(
        on_device,
        mesh=mesh,
        in_specs=placed,
        out_specs=P("tile", None, "stat", None),
        check_vma=False,
    )
```

profile of v0, /device:TPU:1, one launch (start us, length us, event | category | flops | bytes accessed | tf_op | source)
XLA Modules:
  0.0 113.6 jit_solution(15910199022855827285)
XLA Ops:
  6.5 0.0 copy-start.9
  6.5 0.0 copy-start.7
  6.5 0.0 copy-start.2
  6.5 0.0 copy-start.8
  6.5 0.0 copy-start.4
  6.6 0.0 copy-start.5
  6.6 0.0 copy-start.10
  6.6 0.0 copy-start.12
  6.6 0.0 all-gather.2.cloned.1.call-start
  6.6 1.7 %reshape.15 = bf16[32,16,128]{2,1,0:T(8,128)(2,1)} reshape(bf16[32,2,1024]{2,1,0:T(2,128)(2,1)} %param.19) | data formatting | bytes 262144 | tf_op jit(solution)/shard_map/reshape | solution.py:334
  8.4 0.0 all-gather.2.cloned.1.call-update
  8.4 0.8 fusion.16
  9.1 0.1 copy.36
  9.2 0.8 fusion.17
  10.0 0.1 copy.34
  10.1 0.1 copy.35
  10.2 0.1 copy.33
  10.3 0.8 copy.27
  11.2 0.1 concatenate.3.meta_ref
  11.3 0.0 copy-start.3
  11.3 0.9 copy-done.3
  12.2 0.0 copy-start.6
  12.2 0.8 copy-done.6
  13.0 0.0 copy-start.11
  13.0 0.7 copy-done.11
  13.7 1.9 %pack.1 = bf16[32,24,256]{2,1,0:T(8,128)(2,1)} custom-call(s32[32]{0:T(128)S(1)} %bitcast.2, f32[32,8,256]{2,1,0:T(8,128)S(1)} %copy-done.3, f32[32,256]{1,0:T(8,128)S(1)} %copy-done.6, f32[32,256]{1,0:T(8,128)S(1)} %concatenate.3.meta_ref), custom_call_target="tpu_custom_call" | custom-call | tf_op jit(solution)/shard_map/pack/pallas_call | solution.py:266
  15.5 10.5 %all-to-all-start = ((bf16[32,24,256]{2,1,0:T(8,128)(2,1)}), bf16[32,24,256]{2,1,0:T(8,128)(2,1)S(1)}, u32[]{:S(2)}, u32[]{:S(2)}) async-start(bf16[32,24,256]{2,1,0:T(8,128)(2,1)} %pack.1), calls=%async_computation | async-start | bytes 786432 | tf_op jit(solution)/shard_map/all_to_all | solution.py:337
  26.0 0.0 copy-done.12
  26.0 0.1 broadcast_in_dim_tile.3.freq_ref
  26.1 11.5 %all-to-all-done.recv_ref = bf16[32,24,256]{2,1,0:T(8,128)(2,1)S(1)} async-done(((bf16[32,24,256]{2,1,0:T(8,128)(2,1)}), bf16[32,24,256]{2,1,0:T(8,128)(2,1)S(1)}, u32[]{:S(2)}, u32[]{:S(2)}) %all-to-all-start) | async-done | bytes 393248 | tf_op jit(solution)/shard_map/all_to_all | solution.py:337
  37.7 0.1 slice_convert_fusion
  37.8 0.1 reshape.17.ints_ref
  37.9 0.0 copy-done.9
  37.9 0.0 copy-done.7
  37.9 0.0 copy-done.2
  37.9 13.6 %images.1 = (f32[64,32,256]{2,1,0:T(8,128)S(1)}, f32[64,32,256]{2,1,0:T(8,128)S(1)}) custom-call(bf16[32,24,256]{2,1,0:T(8,128)(2,1)S(1)} %all-to-all-done.recv_ref, f32[1,256]{1,0:T(1,128)S(1)} %broadcast_in_dim_tile.3.freq_ref, bf16[4,256,256]{2,1,0:T(8,128)(2,1)S(1)} %copy-done.2, f32[32,256]{1,0:T(8,128)S(1)} %copy-done.7, f32[16,256]{1,0:T(8,128)S(1)} %copy-done.9), custom_call_target="tpu_custom_call" | custom-call | tf_op jit(solution)/shard_map/images/pallas_call | solution.py:280
  51.5 0.0 copy-start
  51.5 1.3 %copy-done = f32[64,32,256]{2,1,0:T(8,128)} copy-done((f32[64,32,256]{2,1,0:T(8,128)}, f32[64,32,256]{2,1,0:T(8,128)S(1)}, u32[]{:S(2)}) %copy-start) | copy-done | bytes 2097176
  52.8 5.9 %all-gather.2.cloned.1.call-done.screen_ref = bf16[512,16,128]{2,1,0:T(8,128)(2,1)} async-done(((bf16[32,16,128]{2,1,0:T(8,128)(2,1)}), bf16[512,16,128]{2,1,0:T(8,128)(2,1)}) %all-gather.2.cloned.1.call-update) | async-done | bytes 2097168 | tf_op jit(solution)/shard_map/all_gather | solution.py:334
  58.8 0.0 copy-done.8
  58.8 0.0 copy-done.4
  58.8 0.0 copy-done.5
  58.8 0.0 copy-done.10
  58.8 0.0 copy-start.1
  58.8 1.6 %copy-done.1 = f32[64,32,256]{2,1,0:T(8,128)S(1)} copy-done((f32[64,32,256]{2,1,0:T(8,128)S(1)}, f32[64,32,256]{2,1,0:T(8,128)}, u32[]{:S(2)}) %copy-start.1) | copy-done | bytes 2097176
  60.4 8.9 %grid_tile.1 = bf16[16,256,128]{2,1,0:T(8,128)(2,1)S(1)} custom-call(s32[512]{0:T(512)S(1)} %reshape.17.ints_ref, f32[64,32,256]{2,1,0:T(8,128)S(1)} %get-tuple-element.7.i_ref, f32[64,32,256]{2,1,0:T(8,128)S(1)} %copy-done.1, bf16[512,16,128]{2,1,0:T(8,128)(2,1)} %all-gather.2.cloned.1.call-done.screen_ref, f32[8,128]{1,0:T(8,128)S(1)} %copy-done.10, ...), custom_call_target="tpu_custom_call" | custom-call | tf_op jit(solution)/shard_map/grid_tile/pallas_call | solution.py:291
  69.3 36.6 %all_to_all.10.in_ref = bf16[16,256,128]{2,1,0:T(8,128)(2,1)S(1)} all-to-all(bf16[16,256,128]{2,1,0:T(8,128)(2,1)S(1)} %grid_tile.1), channel_id=1, replica_groups=mesh['stat'=16,'tile'=32] {'stat'}, dimensions={0} | all-to-all | bytes 2097152 | tf_op jit(solution)/shard_map/all_to_all | solution.py:341
  105.9 0.9 band_sum.1
  (5 shorter events, 0.1 us)
Async XLA Ops:
  6.5 31.3 %copy-start.9 = (f32[16,256]{1,0:T(8,128)S(1)}, f32[16,256]{1,0:T(8,128)}, u32[]{:S(2)}) copy-start(f32[16,256]{1,0:T(8,128)} %constant.90.clone.ycol_ref) | copy-start | bytes 49156
  6.5 31.3 %copy-start.7 = (f32[32,256]{1,0:T(8,128)S(1)}, f32[32,256]{1,0:T(8,128)}, u32[]{:S(2)}) copy-start(f32[32,256]{1,0:T(8,128)} %constant.89.clone.xrow_ref) | copy-start | bytes 98308
  6.5 31.3 %copy-start.2 = (bf16[4,256,256]{2,1,0:T(8,128)(2,1)S(1)}, bf16[4,256,256]{2,1,0:T(8,128)(2,1)}, u32[]{:S(2)}) copy-start(bf16[4,256,256]{2,1,0:T(8,128)(2,1)} %constant.88.clone.spread_ref) | copy-start | bytes 1572868
  6.5 52.2 %copy-start.8 = (bf16[64,64]{1,0:T(8,128)(2,1)S(1)}, bf16[64,64]{1,0:T(8,128)(2,1)}, u32[]{:S(2)}) copy-start(bf16[64,64]{1,0:T(8,128)(2,1)} %constant.94.clone.row_ref) | copy-start | bytes 24580
  6.5 52.2 %copy-start.4 = (bf16[256,256]{1,0:T(8,128)(2,1)S(1)}, bf16[256,256]{1,0:T(8,128)(2,1)}, u32[]{:S(2)}) copy-start(bf16[256,256]{1,0:T(8,128)(2,1)} %constant.93.clone.col_ref) | copy-start | bytes 393220
  6.6 52.2 %copy-start.5 = (bf16[2,128,256]{2,1,0:T(8,128)(2,1)S(1)}, bf16[2,128,256]{2,1,0:T(8,128)(2,1)}, u32[]{:S(2)}) copy-start(bf16[2,128,256]{2,1,0:T(8,128)(2,1)} %constant.92.clone.rep_ref) | copy-start | bytes 393220
  6.6 52.2 %copy-start.10 = (f32[8,128]{1,0:T(8,128)S(1)}, f32[8,128]{1,0:T(8,128)}, u32[]{:S(2)}) copy-start(f32[8,128]{1,0:T(8,128)} %constant.91.clone.taper_ref) | copy-start | bytes 12292
  6.6 19.4 %copy-start.12 = (f32[16]{0:T(128)S(1)}, f32[16]{0:T(128)}, u32[]{:S(2)}) copy-start(f32[16]{0:T(128)} %param.18) | copy-start | bytes 196
  6.6 52.2 %all-gather.2.cloned.1.call-start = ((), (), s32[]{:S(2)}) async-start(), calls=%async_computation.2 | async-start | bytes 2228224 | tf_op jit(solution)/shard_map/all_gather | solution.py:334
  11.3 1.0 copy-start.3
  12.2 0.8 copy-start.6
  13.0 0.7 copy-start.11
  15.5 22.2 %all-to-all-start = ((bf16[32,24,256]{2,1,0:T(8,128)(2,1)}), bf16[32,24,256]{2,1,0:T(8,128)(2,1)S(1)}, u32[]{:S(2)}, u32[]{:S(2)}) async-start(bf16[32,24,256]{2,1,0:T(8,128)(2,1)} %pack.1), calls=%async_computation | async-start | bytes 786432 | tf_op jit(solution)/shard_map/all_to_all | solution.py:337
  51.5 1.3 %copy-start = (f32[64,32,256]{2,1,0:T(8,128)}, f32[64,32,256]{2,1,0:T(8,128)S(1)}, u32[]{:S(2)}) copy-start(f32[64,32,256]{2,1,0:T(8,128)S(1)} %get-tuple-element.8.j_ref) | copy-start | bytes 6291460
  58.8 1.6 %copy-start.1 = (f32[64,32,256]{2,1,0:T(8,128)S(1)}, f32[64,32,256]{2,1,0:T(8,128)}, u32[]{:S(2)}) copy-start(f32[64,32,256]{2,1,0:T(8,128)} %copy-done) | copy-start | bytes 6291460
Sparse Core Ops, SparseCore 0:
  9.5 49.1 all-gather.1
where the time goes:
time: 114 us
  blocking collectives  36.6 us (32%)
  Pallas kernels  25.3 us (22%)
  waiting for transfers between devices  17.5 us (15%)
  between operations  13.6 us (12%)
  starting transfers between devices  10.5 us (9%)
  local copies, waits for them, and re-layouts  9.96 us (9%)
    all_to_all x1, blocking collectives, on_device(): lax.all_to_all(partial, 'stat', split_axis=0, concat_axis=0, tiled=True)  36.6 us
    pallas_call x1, Pallas kernels, images(): call(image_kernel, out_shape=(shape, shape), in_specs=[VM] * 5, out_specs...  13.6 us
    all_to_all x1, waiting for transfers between devices, on_device(): lax.all_to_all(packed, 'tile', split_axis=0, concat_axis=0, tiled=True)  11.5 us
    all_to_all x1, starting transfers between devices, on_device(): lax.all_to_all(packed, 'tile', split_axis=0, concat_axis=0, tiled=True)  10.5 us
    pallas_call x1, Pallas kernels, grid_tile(): call(grid_kernel, out_shape=jax.ShapeDtypeStruct((16, 256, 128), BF16), i...  8.94 us
    all_gather x1, waiting for transfers between devices, on_device(): lax.all_gather(screens.reshape(32, 16, 128), 'stat', axis=0, tiled=True)  5.93 us
    unnamed x30, local copies, waits for them, and re-layouts  5.62 us
  transfers between devices with their start and end apart: 2, of which 2 were waited for; matrix products, arithmetic and copies ran while one was open for 3% of the time, Pallas kernels for 14%

commit v1 on v0

--- a/solution.py
+++ b/solution.py
@@ -7,7 +7,7 @@
 from jax import lax
 from jax.experimental import pallas as pl
 from jax.experimental.pallas import tpu as pltpu
-from jax.sharding import PartitionSpec as P
+from jax.sharding import Mesh, PartitionSpec as P
 
 SUB = 32
 TS = 256
@@ -94,7 +94,41 @@
     return horner(COS_C, s), horner(SIN_C, s) * r
 
 
-def pack_kernel(tile_ref, vis_ref, weight_ref, meta_ref, out_ref, src_ref, count_ref):
+def fetch(pairs, sem):
+    copies = [pltpu.make_async_copy(src, dst, sem.at[i]) for i, (src, dst) in enumerate(pairs)]
+    for copy in copies:
+        copy.start()
+    return copies
+
+
+def pack_kernel(
+    tile_in, vis_in, weight_in, uv_in, station_in, offset_in, out_ref,
+    tile_ref, vis_ref, weight_ref, uv_ref, station_ref, offset_ref, meta_ref, src_ref, count_ref, sem,
+):
+    pairs = (
+        (tile_in, tile_ref), (station_in, station_ref), (offset_in, offset_ref),
+        (uv_in, uv_ref), (weight_in, weight_ref), (vis_in, vis_ref),
+    )
+    copies = fetch(pairs, sem)
+    for copy in copies[:4]:
+        copy.wait()
+    uv = uv_ref[...]
+    hi = uv.astype(BF16)
+    rest = uv - hi.astype(F32)
+    mid = rest.astype(BF16)
+    low = (rest - mid.astype(F32)).astype(BF16)
+    p, q = station_ref[0:1, :], station_ref[1:2, :]
+    r, c = offset_ref[0:1, :], offset_ref[1:2, :]
+    ints = jnp.concatenate([p >> 5, p & 31, q >> 5, q & 31, r >> 3, r & 7, c >> 5, c & 31], axis=0)
+    columns = jnp.concatenate([hi.astype(F32), mid.astype(F32), low.astype(F32), ints.astype(F32)], axis=0)
+    eye = lax.broadcasted_iota(jnp.int32, (104, 256), 0) == lax.broadcasted_iota(jnp.int32, (104, 256), 1)
+    meta_ref[...] = lax.dot_general(
+        columns.astype(BF16),
+        eye.astype(F32).astype(BF16),
+        (((0,), (0,)), ((), ())),
+        preferred_element_type=F32,
+    )
+
     def clear(i, c):
         src_ref[2 * i] = -1
         src_ref[2 * i + 1] = -1
@@ -104,7 +138,7 @@
     lax.fori_loop(0, PEERS, clear, 0, unroll=8)
 
     def assign(s, c):
-        t = tile_ref[s]
+        t = tile_ref[0, s]
         before = count_ref[t]
         src_ref[2 * t + before] = s
         count_ref[t] = before + 1
@@ -112,6 +146,8 @@
 
     lax.fori_loop(0, 32, assign, 0, unroll=4)
     row = lax.broadcasted_iota(jnp.int32, (8, 256), 0)
+    for copy in copies[4:]:
+        copy.wait()
 
     def one_peer(n, c):
         blocks = []
@@ -130,11 +166,31 @@
     lax.fori_loop(0, PEERS, one_peer, 0, unroll=4)
 
 
-def image_kernel(recv_ref, freq_ref, spread_ref, xrow_ref, ycol_ref, i_ref, j_ref, meta_ref, du_ref, dv_ref):
+def image_kernel(
+    recv_ref, freq_in, spread_in, xrow_in, ycol_in, i_ref, ints_out,
+    freq_ref, spread_ref, xrow_ref, ycol_ref, ints_ref, meta_ref, du_ref, dv_ref, sem,
+):
+    pairs = ((freq_in, freq_ref), (spread_in, spread_ref), (xrow_in, xrow_ref), (ycol_in, ycol_ref))
+    copies = fetch(pairs, sem)
     for n in range(PEERS):
         meta_ref[n] = recv_ref[n, 16:24, :].astype(F32)
     meta = meta_ref[...].reshape(256, 256).astype(BF16)
-    freq = freq_ref[...]
+    for copy in copies:
+        copy.wait()
+    pick16 = lax.broadcasted_iota(jnp.int32, (16, 256), 1) % 16 == lax.broadcasted_iota(jnp.int32, (16, 256), 0)
+    freq = jnp.dot(
+        jnp.broadcast_to(freq_ref[...], (8, 16)),
+        pick16.astype(F32),
+        precision=lax.Precision.HIGHEST,
+        preferred_element_type=F32,
+    )[0:1]
+    pick = lax.broadcasted_iota(jnp.int32, (8, 256), 0) + 96 == lax.broadcasted_iota(jnp.int32, (8, 256), 1)
+    ints = lax.dot_general(
+        pick.astype(F32).astype(BF16), meta, (((1,), (1,)), ((), ())), preferred_element_type=F32
+    )
+    ints_ref[...] = ints.astype(jnp.int32)
+    send = pltpu.make_async_copy(ints_ref, ints_out, sem.at[4])
+    send.start()
 
     def spread(k):
         return jnp.dot(meta, spread_ref[k], preferred_element_type=F32)
@@ -164,29 +220,44 @@
             for half, (a, b) in enumerate(((cc + cs, sc + ss), (cc - cs, sc - ss))):
                 image = a + sign * pltpu.roll(b, 64, 1)
                 i_ref[slot, :, 128 * half : 128 * half + 128] = image
-                j_ref[slot, :, 128 * half : 128 * half + 128] = pltpu.roll(image, 64, 1)
         return c
 
     lax.fori_loop(0, PEERS, one_peer, 0)
-
-
-GROUP = 4
-
-
-def grid_kernel(ints_ref, i_ref, j_ref, screen_ref, taper_ref, rep_ref, col_ref, row_ref, out_ref, acc_ref):
+    send.wait()
+
+
+GROUP = 16
+
+
+def grid_kernel(
+    ints_in, i_ref, own_ref, other_ref, taper_in, rep_in, col_in, row_in, keep_ref, give_ref,
+    ints_ref, taper_ref, rep_ref, col_ref, row_ref, acc_ref, sem,
+):
+    pairs = (
+        (ints_in, ints_ref), (taper_in, taper_ref), (rep_in, rep_ref), (col_in, col_ref), (row_in, row_ref),
+    )
+    copies = fetch(pairs, sem)
+    core = lax.axis_index("core")
     acc_ref[...] = jnp.zeros(acc_ref.shape, F32)
+    for copy in copies:
+        copy.wait()
     taper = taper_ref[...]
     lane = lax.broadcasted_iota(jnp.int32, (8, 128), 1)
     sub = lax.broadcasted_iota(jnp.int32, (8, 128), 0)
     cell = lane % 32
     group_mask = [lane // 32 == a for a in range(4)]
 
+    def station(z_core, at):
+        where = (z_core >> 1) * 32 + at
+        mine = (z_core & 1) == core
+        return jnp.where(mine, own_ref[where].astype(F32), other_ref[where].astype(F32))
+
     def one_group(g, c):
         lhs_re, lhs_im = [], []
         for k in range(GROUP):
-            base = (g * GROUP + k) * 8
-            sp = screen_ref[ints_ref[base] * 32 + ints_ref[base + 1]].astype(F32)
-            sq = screen_ref[ints_ref[base + 2] * 32 + ints_ref[base + 3]].astype(F32)
+            at = (g * (GROUP // 2) + k // 2) * 8 + k % 2
+            sp = station(ints_ref[0, at], ints_ref[1, at])
+            sq = station(ints_ref[2, at], ints_ref[3, at])
             pr, pi, qr, qi = sp[:8], sp[8:], sq[:8], sq[8:]
             gain_re = (pr * qr + pi * qi) * taper
             gain_im = (pr * qi - pi * qr) * taper
@@ -195,7 +266,7 @@
         wide_re = jnp.dot(jnp.concatenate(lhs_re, 0).astype(BF16), rep_ref[0], preferred_element_type=F32)
         wide_im = jnp.dot(jnp.concatenate(lhs_im, 0).astype(BF16), rep_ref[1], preferred_element_type=F32)
         image = i_ref[pl.ds(g * GROUP, GROUP)].reshape(GROUP * SUB, 256)
-        swapped = j_ref[pl.ds(g * GROUP, GROUP)].reshape(GROUP * SUB, 256)
+        swapped = jnp.concatenate([pltpu.roll(image[:, :128], 64, 1), pltpu.roll(image[:, 128:], 64, 1)], axis=1)
         corrected = (wide_re * image + wide_im * swapped).astype(BF16)
         half = jnp.dot(corrected, col_ref[...], preferred_element_type=F32).astype(BF16)
         stacked = jnp.concatenate(
@@ -207,9 +278,9 @@
         )
         cells = jnp.dot(row_ref[...], stacked, preferred_element_type=F32)
         for k in range(GROUP):
-            base = (g * GROUP + k) * 8
-            row8, row_shift = ints_ref[base + 4], ints_ref[base + 5]
-            col32, col_shift = ints_ref[base + 6], ints_ref[base + 7]
+            at = (g * (GROUP // 2) + k // 2) * 8 + k % 2
+            row8, row_shift = ints_ref[4, at], ints_ref[5, at]
+            col32, col_shift = ints_ref[6, at], ints_ref[7, at]
             keep_col = cell >= col_shift
             keep_row = sub >= row_shift
             for ri in range(2):
@@ -217,21 +288,24 @@
                     s = cells[ri * 32 + part * 8 : ri * 32 + part * 8 + 8, k * 128 : k * 128 + 128]
                     near = jnp.where(keep_col, s, 0.0)
                     far = s - near
-                    for piece, at in ((near, col32), (far, col32 + 1)):
+                    for piece, block in ((near, col32), (far, col32 + 1)):
                         if part == 0:
                             top = jnp.where(keep_row, piece, 0.0)
-                            acc_ref[ri, at, row8] += top
-                            acc_ref[ri, at, row8 + 4] += piece - top
+                            acc_ref[ri, block, row8] += top
+                            acc_ref[ri, block, row8 + 4] += piece - top
                         else:
-                            acc_ref[ri, at, row8 + part] += piece
+                            acc_ref[ri, block, row8 + part] += piece
         return c
 
     lax.fori_loop(0, SLOTS // GROUP, one_group, 0)
-    for band in range(16):
+    for z in range(8):
         for ri in range(2):
             for a in range(8):
-                piece = acc_ref[ri, a, 2 * band : 2 * band + 2].reshape(16, 128)
-                out_ref[band, (ri * 8 + a) * 16 : (ri * 8 + a) * 16 + 16, :] = piece.astype(BF16)
+                at = (ri * 8 + a) * 16
+                keep = acc_ref[ri, a, pl.ds(4 * z + 2 * core, 2)].reshape(16, 128)
+                give = acc_ref[ri, a, pl.ds(4 * z + 2 - 2 * core, 2)].reshape(16, 128)
+                keep_ref[z, at : at + 16, :] = keep.astype(BF16)
+                give_ref[z, at : at + 16, :] = give.astype(BF16)
 
 
 def sum_kernel(in_ref, out_ref):
@@ -243,7 +317,7 @@
             for a in range(4):
                 at = (ri * 8 + h * 4 + a) * 16
                 total = in_ref[0, at : at + 16, :].astype(F32)
-                for s in range(1, 16):
+                for s in range(1, 8):
                     total = total + in_ref[s, at : at + 16, :].astype(F32)
                 parts.append(total)
             for p in range(4):
@@ -257,54 +331,74 @@
 
 VM = pl.BlockSpec(memory_space=pltpu.VMEM)
 SM = pl.BlockSpec(memory_space=pltpu.SMEM)
+HBM = pl.BlockSpec(memory_space=pltpu.HBM)
 call = functools.partial(
-    pl.pallas_call, compiler_params=pltpu.CompilerParams(vmem_limit_bytes=48 << 20)
+    pl.pallas_call, compiler_params=pltpu.CompilerParams(vmem_limit_bytes=16 << 20)
 )
 
 
-def pack(tile_of, visibilities, weights, meta):
+def pinned(x):
+    return pltpu.with_memory_space_constraint(x, pltpu.HBM)
+
+
+def pack(tile_of, visibilities, weights, uv, stations, offsets):
+    args = (tile_of, visibilities, weights, uv, stations, offsets)
+    args = tuple(pinned(a) for a in args)
     return call(
         pack_kernel,
         out_shape=jax.ShapeDtypeStruct((PEERS, 24, 256), BF16),
-        in_specs=[SM, VM, VM, VM],
+        in_specs=[HBM] * 6,
         out_specs=VM,
-        scratch_shapes=[pltpu.SMEM((SLOTS,), jnp.int32), pltpu.SMEM((PEERS,), jnp.int32)],
+        scratch_shapes=[pltpu.SMEM(tile_of.shape, jnp.int32)]
+        + [pltpu.VMEM(a.shape, a.dtype) for a in args[1:]]
+        + [
+            pltpu.VMEM((32, 256), F32),
+            pltpu.SMEM((SLOTS,), jnp.int32),
+            pltpu.SMEM((PEERS,), jnp.int32),
+            pltpu.SemaphoreType.DMA((6,)),
+        ],
         name="pack",
-    )(tile_of, visibilities, weights, meta)
-
-
-def images(recv, freq_row):
+    )(*args)
+
+
+def images(recv, freq):
     xrow = np.broadcast_to(((ROW_L - 16.0) / SUB)[:, None], (SUB, 256)).astype(np.float32)
     ycol = np.broadcast_to(((np.arange(16) + 0.5) / SUB)[:, None], (16, 256)).astype(np.float32)
-    shape = jax.ShapeDtypeStruct((SLOTS, SUB, 256), F32)
+    args = (freq, jnp.asarray(spread_tables(), BF16), jnp.asarray(xrow), jnp.asarray(ycol))
     return call(
         image_kernel,
-        out_shape=(shape, shape),
-        in_specs=[VM] * 5,
-        out_specs=(VM, VM),
-        scratch_shapes=[pltpu.VMEM((PEERS, 8, 256), F32)] * 3,
+        out_shape=(
+            jax.ShapeDtypeStruct((SLOTS, SUB, 256), F32),
+            jax.ShapeDtypeStruct((8, 256), jnp.int32),
+        ),
+        in_specs=[VM] + [HBM] * 4,
+        out_specs=(VM, HBM),
+        scratch_shapes=[pltpu.VMEM(a.shape, a.dtype) for a in args]
+        + [pltpu.VMEM((8, 256), jnp.int32)]
+        + [pltpu.VMEM((PEERS, 8, 256), F32)] * 3
+        + [pltpu.SemaphoreType.DMA((5,))],
         name="images",
-    )(recv, freq_row, jnp.asarray(spread_tables(), BF16), jnp.asarray(xrow), jnp.asarray(ycol))
-
-
-def grid_tile(ints, image, swapped, screens):
-    return call(
-        grid_kernel,
-        out_shape=jax.ShapeDtypeStruct((16, 256, 128), BF16),
-        in_specs=[SM] + [VM] * 7,
-        out_specs=VM,
-        scratch_shapes=[pltpu.VMEM((2, 9, 33, 8, 128), F32)],
-        name="grid_tile",
-    )(
-        ints,
-        image,
-        swapped,
-        screens,
+    )(recv, *[pinned(a) for a in args])
+
+
+def grid_tile(ints, image, own, other):
+    shape = jax.ShapeDtypeStruct((8, 256, 128), BF16)
+    tables = (
         jnp.asarray(taper_table()),
         jnp.asarray(replicate_tables(), BF16),
         jnp.asarray(column_table(), BF16),
         jnp.asarray(row_table(), BF16),
     )
+    return call(
+        grid_kernel,
+        out_shape=(shape, shape),
+        in_specs=[HBM, VM, VM, VM] + [HBM] * 4,
+        out_specs=(VM, VM),
+        scratch_shapes=[pltpu.SMEM(ints.shape, jnp.int32)]
+        + [pltpu.VMEM(t.shape, t.dtype) for t in tables]
+        + [pltpu.VMEM((2, 9, 33, 8, 128), F32), pltpu.SemaphoreType.DMA((5,))],
+        name="grid_tile",
+    )(pinned(ints), image, own, other, *[pinned(t) for t in tables])
 
 
 def band_sum(arrived):
@@ -317,46 +411,43 @@
     )(arrived)
 
 
-def make_meta(uv_coords, stations, offsets):
-    uv = uv_coords.reshape(32, 32)
-    hi = lax.reduce_precision(uv, 8, 7)
-    mid = lax.reduce_precision(uv - hi, 8, 7)
-    low = (uv - hi) - mid
-    p, q = stations[:, 0:1], stations[:, 1:2]
-    r, c = offsets[:, 0:1], offsets[:, 1:2]
-    ints = [p // 32, p % 32, q // 32, q % 32, r // 8, r % 8, c // 32, c % 32]
-    return jnp.concatenate(
-        [hi, mid, low] + [i.astype(F32) for i in ints] + [jnp.zeros((32, 152), F32)], axis=1
-    )
+SWAP = [(0, 1), (1, 0)]
 
 
 def on_device(visibilities, weights, uv_coords, freq_ratio, screens, stations, offsets, tile_ids):
-    everyone = lax.all_gather(screens.reshape(32, 16, 128), "stat", axis=0, tiled=True)
-    meta = make_meta(uv_coords, stations, offsets)
-    packed = pack(tile_ids[:, 0], visibilities, weights, meta)
+    uv = jnp.transpose(uv_coords, (1, 2, 0)).reshape(32, 32)
+    packed = pack(tile_ids.T, visibilities, weights, uv, stations.T, offsets.T)
     recv = lax.all_to_all(packed, "tile", split_axis=0, concat_axis=0, tiled=True)
-    ints = recv[:, 16:18, 96:104].astype(jnp.int32).reshape(SLOTS * 8)
-    image, swapped = images(recv, jnp.tile(freq_ratio, 16)[None, :])
-    partial = grid_tile(ints, image, swapped, everyone)
-    arrived = lax.all_to_all(partial, "stat", split_axis=0, concat_axis=0, tiled=True)
+    mine = jnp.broadcast_to(screens.reshape(1, 32, 16, 128), (8, 32, 16, 128))
+    own = lax.all_to_all(mine, "z", split_axis=0, concat_axis=0, tiled=True).reshape(256, 16, 128)
+    image, ints = images(recv, freq_ratio[None, :])
+    own, image = lax.optimization_barrier((own, image))
+    other = lax.ppermute(own, "core", SWAP)
+    keep, give = grid_tile(ints, image, own, other)
+    taken = lax.ppermute(give, "core", SWAP)
+    both = (keep.astype(F32) + taken.astype(F32)).astype(BF16)
+    arrived = lax.all_to_all(both, "z", split_axis=0, concat_axis=0, tiled=True)
     return band_sum(arrived)
 
 
 def solution(mesh):
+    stat, tile = mesh.shape["stat"], mesh.shape["tile"]
+    fine = Mesh(mesh.devices.reshape(stat // 2, 2, tile), ("z", "core", "tile"))
+    every = ("z", "core", "tile")
     placed = (
-        P(("stat", "tile"), None, None),
-        P(("stat", "tile"), None),
-        P(("stat", "tile"), None, None),
+        P(every, None, None),
+        P(every, None),
+        P(every, None, None),
         P(),
-        P("stat", None, None),
-        P(("stat", "tile"), None),
-        P(("stat", "tile"), None),
-        P(("stat", "tile"), None),
+        P(("z", "core"), None, None),
+        P(every, None),
+        P(every, None),
+        P(every, None),
     )
     return jax.shard_map(
         on_device,
-        mesh=mesh,
+        mesh=fine,
         in_specs=placed,
-        out_specs=P("tile", None, "stat", None),
+        out_specs=P("tile", None, ("z", "core"), None),
         check_vma=False,
     )

time: 114 us -> 99.7 us (0.87)
  starting transfers between devices: 10.5 us -> 28.8 us
  blocking collectives: 36.6 us -> 20.4 us
  between operations: 13.6 us -> 0.07 us
  waiting for transfers between devices: 17.5 us -> 26.7 us
  local copies, waits for them, and re-layouts: 9.96 us -> 2.69 us
  Pallas kernels: 25.3 us -> 19.5 us
    all_to_all x1, blocking collectives: 36.6 us -> 20.4 us  [on_device(): arrived = lax.all_to_all(both, 'z', split_axis=0, concat_axis=0, tiled=True)]
    all_to_all x0 -> x1, waiting for transfers between devices: none -> 12.2 us  [on_device(): lax.all_to_all(mine, 'z', split_axis=0, concat_axis=0, tiled=True)]
    all_to_all x0 -> x1, starting transfers between devices: none -> 10 us  [on_device(): lax.all_to_all(mine, 'z', split_axis=0, concat_axis=0, tiled=True)]
    ppermute x0 -> x2, starting transfers between devices: none -> 8.26 us  [the longest x1 5.99 us: on_device(): other = lax.ppermute(own, 'core', SWAP)]
    pallas_call x2, Pallas kernels: 22.6 us -> 16.5 us  [the longest x1 12.8 us: images(): call(image_kernel, out_shape=(jax.ShapeDtypeStruct((SLOTS, SUB, 256), F32...]
    all_gather x1 -> x0, waiting for transfers between devices: 5.93 us -> none  [on_device(): lax.all_gather(screens.reshape(32, 16, 128), 'stat', axis=0, tiled=True)]
    unnamed x30 -> x2, local copies, waits for them, and re-layouts: 5.62 us -> 0.59 us
    ppermute x0 -> x2, waiting for transfers between devices: none -> 3.79 us  [the longest x1 2.26 us: on_device(): other = lax.ppermute(own, 'core', SWAP)]
  transfers between devices with their start and end apart: 2 -> 4, of which waited for: 2 -> 4; matrix products, arithmetic and copies ran while one was open for 3% -> 1% of each run, Pallas kernels for 14% -> 13%
where the time goes in v1:
time: 99.7 us; the launch traced here: 98.2 us
  starting transfers between devices  28.8 us (29%)
  waiting for transfers between devices  26.7 us (27%)
  blocking collectives  20.4 us (20%)
  Pallas kernels  19.5 us (20%)
  local copies, waits for them, and re-layouts  2.69 us (3%)
    all_to_all x1, blocking collectives, on_device(): arrived = lax.all_to_all(both, 'z', split_axis=0, concat_axis=0, tiled=True)  20.4 us
    pallas_call x1, Pallas kernels, images(): call(image_kernel, out_shape=(jax.ShapeDtypeStruct((SLOTS, SUB, 256), F32...  12.8 us
    all_to_all x1, waiting for transfers between devices, on_device(): lax.all_to_all(mine, 'z', split_axis=0, concat_axis=0, tiled=True)  12.2 us
    all_to_all x1, waiting for transfers between devices, on_device(): lax.all_to_all(packed, 'tile', split_axis=0, concat_axis=0, tiled=True)  10.6 us
    all_to_all x1, starting transfers between devices, on_device(): lax.all_to_all(packed, 'tile', split_axis=0, concat_axis=0, tiled=True)  10.5 us
    all_to_all x1, starting transfers between devices, on_device(): lax.all_to_all(mine, 'z', split_axis=0, concat_axis=0, tiled=True)  10 us
    ppermute x1, starting transfers between devices, on_device(): other = lax.ppermute(own, 'core', SWAP)  5.99 us
    pallas_call x1, Pallas kernels, grid_tile(): call(grid_kernel, out_shape=(shape, shape), in_specs=[HBM, VM, VM, VM] +...  3.71 us
  transfers between devices with their start and end apart: 4, of which 4 were waited for; matrix products, arithmetic and copies ran while one was open for 1% of the time, Pallas kernels for 13%

profile of v1, /device:TPU:1, one launch (start us, length us, event | category | flops | bytes accessed | tf_op | source)
XLA Modules:
  0.0 98.2 jit_solution(10968002637429467545)
XLA Ops:
  0.0 2.1 %pack.1 = bf16[32,24,256]{2,1,0:T(8,128)(2,1)} custom-call(s32[1,32]{1,0:T(1,128)} %bitcast.14, f32[32,8,256]{2,1,0:T(8,128)} %vis_in.1, f32[32,256]{1,0:T(8,128)} %weight_in.1, f32[32,32]{1,0:T(8,128)} %bitcast.10, s32[2,32]{1,0:T(2,128)} %bitcast.11, s32[2,32]{1,0:T(2,128)} %bitcast.12), custom_call_target="tpu_custom_call" | custom-call | tf_op jit(solution)/shard_map/pack/pallas_call | solution.py:347
  2.1 10.5 %all-to-all-start = ((bf16[32,24,256]{2,1,0:T(8,128)(2,1)}), bf16[32,24,256]{2,1,0:T(8,128)(2,1)S(1)}, u32[]{:S(2)}, u32[]{:S(2)}) async-start(bf16[32,24,256]{2,1,0:T(8,128)(2,1)} %pack.1), calls=%async_computation | async-start | bytes 786432 | tf_op jit(solution)/shard_map/all_to_all | solution.py:420
  12.7 1.0 %broadcast_in_dim.11 = bf16[32,16,128]{2,1,0:T(8,128)(2,1)S(1)} reshape(bf16[32,2,1024]{2,1,0:T(2,128)(2,1)} %param.19) | data formatting | bytes 262144 | tf_op jit(solution)/shard_map/broadcast_in_dim | solution.py:421
  13.7 10.6 %all-to-all-done.recv_ref = bf16[32,24,256]{2,1,0:T(8,128)(2,1)S(1)} async-done(((bf16[32,24,256]{2,1,0:T(8,128)(2,1)}), bf16[32,24,256]{2,1,0:T(8,128)(2,1)S(1)}, u32[]{:S(2)}, u32[]{:S(2)}) %all-to-all-start) | async-done | bytes 393248 | tf_op jit(solution)/shard_map/all_to_all | solution.py:420
  24.3 1.1 %broadcast_in_dim.12 = bf16[8,32,16,128]{3,2,1,0:T(8,128)(2,1)} broadcast(bf16[32,16,128]{2,1,0:T(8,128)(2,1)S(1)} %broadcast_in_dim.11), dimensions={1,2,3} | broadcast | bytes 1179648 | tf_op jit(solution)/shard_map/broadcast_in_dim | solution.py:421
  25.4 10.0 %all-to-all-start.1 = ((bf16[8,32,16,128]{3,2,1,0:T(8,128)(2,1)}), bf16[8,32,16,128]{3,2,1,0:T(8,128)(2,1)S(1)}, u32[]{:S(2)}, u32[]{:S(2)}) async-start(bf16[8,32,16,128]{3,2,1,0:T(8,128)(2,1)} %broadcast_in_dim.12), calls=%async_computation.1 | async-start | bytes 2097152 | tf_op jit(solution)/shard_map/all_to_all | solution.py:422
  35.4 12.8 %images.1 = (f32[64,32,256]{2,1,0:T(8,128)S(1)}, s32[8,256]{1,0:T(8,128)S(1)}) custom-call(bf16[32,24,256]{2,1,0:T(8,128)(2,1)S(1)} %all-to-all-done.recv_ref, f32[1,16]{1,0:T(1,128)} %bitcast.13, bf16[4,256,256]{2,1,0:T(8,128)(2,1)} %constant.14.clone.spread_in, f32[32,256]{1,0:T(8,128)} %constant.15.clone.xrow_in, f32[16,256]{1,0:T(8,128)} %constant.16.clone.ycol_in), custom_call_target="tpu_custom_call" | custom-call | tf_op jit(solution)/shard_map/images/pallas_call | solution.py:368
  48.2 0.0 copy-start
  48.3 0.6 copy-done
  48.9 12.2 %all-to-all-done.1 = bf16[8,32,16,128]{3,2,1,0:T(8,128)(2,1)S(1)} async-done(((bf16[8,32,16,128]{3,2,1,0:T(8,128)(2,1)}), bf16[8,32,16,128]{3,2,1,0:T(8,128)(2,1)S(1)}, u32[]{:S(2)}, u32[]{:S(2)}) %all-to-all-start.1) | async-done | bytes 1048608 | tf_op jit(solution)/shard_map/all_to_all | solution.py:422
  61.1 6.0 %collective-permute-start = (bf16[256,16,128]{2,1,0:T(8,128)(2,1)S(1)}, bf16[256,16,128]{2,1,0:T(8,128)(2,1)S(1)}, u32[]{:S(2)}, u32[]{:S(2)}) collective-permute-start(bf16[256,16,128]{2,1,0:T(8,128)(2,1)S(1)} %bitcast.8), channel_id=1, source_target_pairs={{0,32},{32,0},{1,33},{33,1},{2,34},{34,2},{3,35},{35,3},{4,36},{36... | collective-permute-start | bytes 3145736 | tf_op jit(solution)/shard_map/ppermute | solution.py:425
  67.1 2.3 %collective-permute-done.other_ref = bf16[256,16,128]{2,1,0:T(8,128)(2,1)S(1)} collective-permute-done((bf16[256,16,128]{2,1,0:T(8,128)(2,1)S(1)}, bf16[256,16,128]{2,1,0:T(8,128)(2,1)S(1)}, u32[]{:S(2)}, u32[]{:S(2)}) %collective-permute-start) | collective-permute-done | bytes 1048608 | tf_op jit(solution)/shard_map/ppermute | solution.py:425
  69.3 3.7 %grid_tile.1 = (bf16[8,256,128]{2,1,0:T(8,128)(2,1)S(1)}, bf16[8,256,128]{2,1,0:T(8,128)(2,1)S(1)}) custom-call(s32[8,256]{1,0:T(8,128)} %copy-done, f32[64,32,256]{2,1,0:T(8,128)S(1)} %get-tuple-element.13.i_ref, bf16[256,16,128]{2,1,0:T(8,128)(2,1)S(1)} %bitcast.9, bf16[256,16,128]{2,1,0:T(8,128)(2,1)S(1)} %collective-permute-done.other_ref, ...), custom_call_target="tpu_custom_call" | custom-call | tf_op jit(solution)/shard_map/grid_tile/pallas_call | solution.py:392
  73.1 2.3 %collective-permute-start.1 = (bf16[8,256,128]{2,1,0:T(8,128)(2,1)S(1)}, bf16[8,256,128]{2,1,0:T(8,128)(2,1)S(1)}, u32[]{:S(2)}, u32[]{:S(2)}) collective-permute-start(bf16[8,256,128]{2,1,0:T(8,128)(2,1)S(1)} %get-tuple-element.16), channel_id=1, source_target_pairs={{0,32},{32,0},{1,33},{33,1},{2,34},{34,2},{3,35},{35,3},{4,36},{36... | collective-permute-start | bytes 1572872 | tf_op jit(solution)/shard_map/ppermute | solution.py:427
  75.3 1.5 %collective-permute-done.1 = bf16[8,256,128]{2,1,0:T(8,128)(2,1)S(1)} collective-permute-done((bf16[8,256,128]{2,1,0:T(8,128)(2,1)S(1)}, bf16[8,256,128]{2,1,0:T(8,128)(2,1)S(1)}, u32[]{:S(2)}, u32[]{:S(2)}) %collective-permute-start.1) | collective-permute-done | bytes 524320 | tf_op jit(solution)/shard_map/ppermute | solution.py:427
  76.9 0.1 add_convert_fusion
  77.0 20.4 %all_to_all.15.in_ref = bf16[8,256,128]{2,1,0:T(8,128)(2,1)S(1)} all-to-all(bf16[8,256,128]{2,1,0:T(8,128)(2,1)S(1)} %add_convert_fusion), channel_id=1, replica_groups=mesh['z'=8,'core'=2,'tile'=32] {'z'}, dimensions={0} | all-to-all | bytes 1048576 | tf_op jit(solution)/shard_map/all_to_all | solution.py:429
  97.4 0.8 band_sum.1
Async XLA Ops:
  2.1 22.2 %all-to-all-start = ((bf16[32,24,256]{2,1,0:T(8,128)(2,1)}), bf16[32,24,256]{2,1,0:T(8,128)(2,1)S(1)}, u32[]{:S(2)}, u32[]{:S(2)}) async-start(bf16[32,24,256]{2,1,0:T(8,128)(2,1)} %pack.1), calls=%async_computation | async-start | bytes 786432 | tf_op jit(solution)/shard_map/all_to_all | solution.py:420
  25.4 35.7 %all-to-all-start.1 = ((bf16[8,32,16,128]{3,2,1,0:T(8,128)(2,1)}), bf16[8,32,16,128]{3,2,1,0:T(8,128)(2,1)S(1)}, u32[]{:S(2)}, u32[]{:S(2)}) async-start(bf16[8,32,16,128]{3,2,1,0:T(8,128)(2,1)} %broadcast_in_dim.12), calls=%async_computation.1 | async-start | bytes 2097152 | tf_op jit(solution)/shard_map/all_to_all | solution.py:422
  48.2 0.6 copy-start
  61.1 8.3 %collective-permute-start = (bf16[256,16,128]{2,1,0:T(8,128)(2,1)S(1)}, bf16[256,16,128]{2,1,0:T(8,128)(2,1)S(1)}, u32[]{:S(2)}, u32[]{:S(2)}) collective-permute-start(bf16[256,16,128]{2,1,0:T(8,128)(2,1)S(1)} %bitcast.8), channel_id=1, source_target_pairs={{0,32},{32,0},{1,33},{33,1},{2,34},{34,2},{3,35},{35,3},{4,36},{36... | collective-permute-start | bytes 3145736 | tf_op jit(solution)/shard_map/ppermute | solution.py:425
  73.1 3.8 %collective-permute-start.1 = (bf16[8,256,128]{2,1,0:T(8,128)(2,1)S(1)}, bf16[8,256,128]{2,1,0:T(8,128)(2,1)S(1)}, u32[]{:S(2)}, u32[]{:S(2)}) collective-permute-start(bf16[8,256,128]{2,1,0:T(8,128)(2,1)S(1)} %get-tuple-element.16), channel_id=1, source_target_pairs={{0,32},{32,0},{1,33},{33,1},{2,34},{34,2},{3,35},{35,3},{4,36},{36... | collective-permute-start | bytes 1572872 | tf_op jit(solution)/shard_map/ppermute | solution.py:427

commit v2 on v1

v2 whole, which is shorter than its diff:
```python
import functools
import math

import jax
import jax.numpy as jnp
import numpy as np
from jax import lax
from jax.experimental import pallas as pl
from jax.experimental.pallas import tpu as pltpu
from jax.sharding import Mesh, PartitionSpec as P

SUB = 32
TS = 256
K = 256
SLOTS = 64
PEERS = 32
F32 = jnp.float32
BF16 = jnp.bfloat16

ROW_L = np.array([4 * (r % 8) + r // 8 for r in range(SUB)])
LANE = np.arange(128)
LANE_I = LANE % 16
LANE_P = (LANE // 16) % 2
LANE_RI = LANE // 64
LANE_M = np.where((LANE // 32) % 2 == 0, 16 + LANE_I, 15 - LANE_I)


def spread_tables():
    out = np.zeros((4, 256, 256), np.float32)
    for part in range(3):
        for t in range(16):
            out[0, part * 32 + t, t * 16 : (t + 1) * 16] = 1.0
            out[1, part * 32 + 16 + t, t * 16 : (t + 1) * 16] = 1.0
    out[2, 101, :] = 1.0
    out[3, 103, :] = 1.0
    return out


def replicate_tables():
    cell = np.arange(128) % 32
    rep = (cell[:, None] == LANE_M[None, :]).astype(np.float32)
    sign = np.where(LANE_RI == 0, -1.0, 1.0).astype(np.float32)
    return np.stack([rep, rep * sign[None, :]])


def column_table():
    n = np.arange(256)
    twice, ri, p, v = n // 128, (n // 64) % 2, (n // 32) % 2, n % 32
    turns = -(LANE_M[:, None] - 16.0) * (v[None, :] - 16.0) / SUB
    turns = turns + 0.25 * (twice[None, :] - ri[None, :] + LANE_RI[:, None])
    val = np.cos(2.0 * np.pi * turns)
    return np.where(LANE_P[:, None] == p[None, :], val, 0.0)


def row_table():
    u, part, l = np.arange(32), np.arange(64) // 32, ROW_L[np.arange(64) % 32]
    angle = -2.0 * np.pi / SUB * (u[:, None] - 16.0) * (l[None, :] - 16.0)
    return np.where(part[None, :] == 0, np.cos(angle), np.sin(angle))


def taper_table():
    flat = np.arange(1024)
    l, m = flat // 32, flat % 32
    one = np.sin(np.pi * (np.arange(SUB) + 0.5) / SUB)
    return (one[l] * one[m] / (K * SUB)).reshape(8, 128).astype(np.float32)


def fit_turns():
    s = (0.5 * np.cos(np.pi * (np.arange(400) + 0.5) / 800)) ** 2
    r = np.sqrt(s)
    cheb = np.polynomial.chebyshev.Chebyshev.fit
    cos = cheb(s, np.cos(2 * np.pi * r), 6, domain=[0, 0.25]).convert(kind=np.polynomial.Polynomial)
    sin = cheb(s, np.sin(2 * np.pi * r) / r, 5, domain=[0, 0.25]).convert(kind=np.polynomial.Polynomial)
    return [float(c) for c in cos.coef], [float(c) for c in sin.coef]


COS_C, SIN_C = fit_turns()


def horner(coef, s):
    acc = jnp.full_like(s, coef[-1])
    for c in coef[-2::-1]:
        acc = acc * s + c
    return acc


def cos_sin_turns(turns):
    r = turns - jnp.round(turns)
    s = r * r
    return horner(COS_C, s), horner(SIN_C, s) * r


def fetch(pairs, sem):
    copies = [pltpu.make_async_copy(src, dst, sem.at[i]) for i, (src, dst) in enumerate(pairs)]
    for copy in copies:
        copy.start()
    return copies


def pack_kernel(
    tile_in, vis_in, weight_in, uv_in, station_in, offset_in, screen_in, out_ref, mine_out,
    tile_ref, vis_ref, weight_ref, uv_ref, station_ref, offset_ref, screen_ref,
    meta_ref, wide_ref, mine_ref, src_ref, count_ref, sem,
):
    pairs = (
        (tile_in, tile_ref), (station_in, station_ref), (offset_in, offset_ref),
        (uv_in, uv_ref), (weight_in, weight_ref), (vis_in, vis_ref), (screen_in, screen_ref),
    )
    copies = fetch(pairs, sem)
    for copy in copies[:4]:
        copy.wait()
    uv = uv_ref[...]
    hi = uv.astype(BF16)
    rest = uv - hi.astype(F32)
    mid = rest.astype(BF16)
    low = (rest - mid.astype(F32)).astype(BF16)
    p, q = station_ref[0:1, :], station_ref[1:2, :]
    r, c = offset_ref[0:1, :], offset_ref[1:2, :]
    ints = jnp.concatenate([p >> 5, p & 31, q >> 5, q & 31, r >> 3, r & 7, c >> 5, c & 31], axis=0)
    columns = jnp.concatenate([hi.astype(F32), mid.astype(F32), low.astype(F32), ints.astype(F32)], axis=0)
    eye = lax.broadcasted_iota(jnp.int32, (104, 256), 0) == lax.broadcasted_iota(jnp.int32, (104, 256), 1)
    meta_ref[...] = lax.dot_general(
        columns.astype(BF16),
        eye.astype(F32).astype(BF16),
        (((0,), (0,)), ((), ())),
        preferred_element_type=F32,
    )

    def clear(i, c):
        src_ref[2 * i] = -1
        src_ref[2 * i + 1] = -1
        count_ref[i] = 0
        return c

    lax.fori_loop(0, PEERS, clear, 0, unroll=8)

    def assign(s, c):
        t = tile_ref[0, s]
        before = count_ref[t]
        src_ref[2 * t + before] = s
        count_ref[t] = before + 1
        return c

    lax.fori_loop(0, 32, assign, 0, unroll=4)
    row = lax.broadcasted_iota(jnp.int32, (8, 256), 0)
    for copy in copies[4:6]:
        copy.wait()

    def one_peer(n, c):
        low, high = [], []
        meta = jnp.zeros((8, 256), F32)
        for j in range(2):
            s = src_ref[2 * n + j]
            valid = s >= 0
            at = jnp.maximum(s, 0)
            weighted = jnp.where(valid, vis_ref[at] * weight_ref[pl.ds(at, 1), :], 0.0)
            low += [weighted[0:2], weighted[4:6]]
            high += [weighted[2:4], weighted[6:8]]
            meta = jnp.where(jnp.logical_and(row == j, valid), meta_ref[pl.ds(at, 1), :], meta)
        out_ref[n] = jnp.concatenate(low + high + [meta], axis=0).astype(BF16)
        return c

    lax.fori_loop(0, PEERS, one_peer, 0, unroll=4)
    copies[6].wait()
    wide_ref[...] = screen_ref[...].astype(F32).reshape(512, 128)
    parts = [wide_ref[pl.ds(ri, 256, stride=2), :].reshape(32, 8, 128) for ri in range(2)]
    mine_ref[...] = jnp.concatenate(parts, axis=1).astype(BF16)
    sends = fetch([(mine_ref, mine_out.at[z]) for z in range(8)], sem)
    for send in sends:
        send.wait()


def image_kernel(
    recv_ref, other_ref, freq_in, spread_in, xrow_in, ycol_in, i_ref, ints_out,
    freq_ref, spread_ref, xrow_ref, ycol_ref, ints_ref, meta_ref, du_ref, dv_ref, sem,
):
    pairs = ((freq_in, freq_ref), (spread_in, spread_ref), (xrow_in, xrow_ref), (ycol_in, ycol_ref))
    copies = fetch(pairs, sem)
    core = lax.axis_index("core")
    for b, block_ref in enumerate((recv_ref, other_ref)):
        for n in range(PEERS):
            meta_ref[b * PEERS + n] = block_ref[3 * n + 2].astype(F32)
    meta = meta_ref[...].reshape(512, 256).astype(BF16)
    for copy in copies:
        copy.wait()
    pick16 = lax.broadcasted_iota(jnp.int32, (16, 256), 1) % 16 == lax.broadcasted_iota(jnp.int32, (16, 256), 0)
    freq = jnp.dot(
        jnp.broadcast_to(freq_ref[...], (8, 16)),
        pick16.astype(F32),
        precision=lax.Precision.HIGHEST,
        preferred_element_type=F32,
    )[0:1]
    pick = lax.broadcasted_iota(jnp.int32, (8, 256), 0) + 96 == lax.broadcasted_iota(jnp.int32, (8, 256), 1)
    ints = lax.dot_general(
        pick.astype(F32).astype(BF16), meta, (((1,), (1,)), ((), ())), preferred_element_type=F32
    )
    ints_ref[...] = ints.astype(jnp.int32)
    send = pltpu.make_async_copy(ints_ref, ints_out, sem.at[4])
    send.start()

    def spread(k):
        return jnp.dot(meta, spread_ref[k], preferred_element_type=F32)

    du_ref[...] = (spread(0) * freq + spread(2)).reshape(2 * PEERS, 8, 256)
    dv_ref[...] = (spread(1) * freq + spread(3)).reshape(2 * PEERS, 8, 256)

    def one_slot(block_ref, row, n, j, slot):
        du = du_ref[row, j : j + 1, :]
        dv = dv_ref[row, j : j + 1, :]
        cu, su = cos_sin_turns(xrow_ref[...] * du - dv * (0.5 / SUB))
        cv, sv = cos_sin_turns(ycol_ref[...] * dv)
        left = jnp.concatenate([cu.astype(BF16), su.astype(BF16)], axis=1)
        w = block_ref[3 * n + core].astype(F32)[4 * j : 4 * j + 4, :]
        table = {}
        for p in range(2):
            re, im = w[p : p + 1, :], w[2 + p : 3 + p, :]
            for ri, (a, b) in enumerate(((re * cv, im * sv), (im * cv, re * sv))):
                minus, plus = (a - b).astype(BF16), (a + b).astype(BF16)
                table[ri, 0, p] = minus if ri == 0 else plus
                table[ri, 1, p] = plus if ri == 0 else minus
        keys = [(ri, s, p) for ri in range(2) for s in range(2) for p in range(2)]
        direct = jnp.concatenate([table[key] for key in keys], axis=0)
        turned = jnp.concatenate([-table[1, s, p] if ri == 0 else table[0, s, p] for ri, s, p in keys], axis=0)
        right = jnp.concatenate([direct, turned], axis=1)
        i_ref[slot] = lax.dot_general(left, right, (((1,), (1,)), ((), ())), preferred_element_type=F32)

    def one_peer(n, c):
        for b, block_ref in enumerate((recv_ref, other_ref)):
            for j in range(2):
                one_slot(block_ref, b * PEERS + n, n, j, 4 * n + 2 * b + j)
        return c

    lax.fori_loop(0, PEERS, one_peer, 0, unroll=2)
    send.wait()


GROUP = 32


def grid_kernel(
    ints_in, i_ref, own_ref, other_ref, taper_in, rep_in, col_in, row_in, out_ref,
    ints_ref, taper_ref, rep_ref, col_ref, row_ref, acc_ref, sem,
):
    pairs = (
        (ints_in, ints_ref), (taper_in, taper_ref), (rep_in, rep_ref), (col_in, col_ref), (row_in, row_ref),
    )
    copies = fetch(pairs, sem)
    core = lax.axis_index("core")
    acc_ref[...] = jnp.zeros(acc_ref.shape, F32)
    for copy in copies:
        copy.wait()
    taper = taper_ref[...]
    lane = lax.broadcasted_iota(jnp.int32, (8, 128), 1)
    sub = lax.broadcasted_iota(jnp.int32, (8, 128), 0)
    cell = lane % 32
    lane16 = lax.broadcasted_iota(jnp.int32, (16, 128), 1) // 32
    upper = lax.broadcasted_iota(jnp.int32, (16, 128), 0) // 8
    group_mask = [(lane16 == 2 * a + upper).astype(F32).astype(BF16) for a in range(2)]

    def station(z_core, at):
        where = (z_core >> 1) * 32 + at
        mine = (z_core & 1) == core
        return jnp.where(mine, own_ref[where], other_ref[where]).astype(F32)

    def place(g, k):
        return (k // 2 % 2) * 256 + (g * (GROUP // 4) + k // 4) * 8 + k % 2

    def one_group(g, c):
        lhs_re, lhs_im = [], []
        for k in range(GROUP):
            at = place(g, k)
            sp = station(ints_ref[0, at], ints_ref[1, at])
            sq = station(ints_ref[2, at], ints_ref[3, at])
            pr, pi, qr, qi = sp[:8], sp[8:], sq[:8], sq[8:]
            gain_re = (pr * qr + pi * qi) * taper
            gain_im = (pr * qi - pi * qr) * taper
            twice_re = jnp.concatenate([gain_re, gain_re], 0).astype(BF16)
            twice_im = jnp.concatenate([gain_im, gain_im], 0).astype(BF16)
            lhs_re += [twice_re * m for m in group_mask]
            lhs_im += [twice_im * m for m in group_mask]
        wide_re = jnp.dot(jnp.concatenate(lhs_re, 0), rep_ref[0], preferred_element_type=F32)
        wide_im = jnp.dot(jnp.concatenate(lhs_im, 0), rep_ref[1], preferred_element_type=F32)
        image = i_ref[pl.ds(g * GROUP, GROUP)].reshape(GROUP * SUB, 128)
        swapped = pltpu.roll(image, 64, 1)
        corrected = (wide_re * image + wide_im * swapped).astype(BF16)
        half = jnp.dot(corrected, col_ref[...], preferred_element_type=F32).astype(BF16)
        stacked = jnp.concatenate(
            [
                jnp.concatenate([half[k * 32 : k * 32 + 32, :128], half[k * 32 : k * 32 + 32, 128:]], axis=0)
                for k in range(GROUP)
            ],
            axis=1,
        )
        cells = jnp.dot(row_ref[...], stacked, preferred_element_type=F32)
        for k in range(GROUP):
            at = place(g, k)
            row8, row_shift = ints_ref[4, at], ints_ref[5, at]
            col32, col_shift = ints_ref[6, at], ints_ref[7, at]
            keep_col = cell >= col_shift
            keep_row = sub >= row_shift
            for part in range(4):
                s = cells[part * 8 : part * 8 + 8, k * 128 : k * 128 + 128]
                near = jnp.where(keep_col, s, 0.0)
                far = s - near
                for piece, block in ((near, col32), (far, col32 + 1)):
                    if part == 0:
                        top = jnp.where(keep_row, piece, 0.0)
                        acc_ref[block, row8] += top
                        acc_ref[block, row8 + 4] += piece - top
                    else:
                        acc_ref[block, row8 + part] += piece
        return c

    lax.fori_loop(0, 2 * SLOTS // GROUP, one_group, 0)
    for band in range(16):
        for a in range(8):
            piece = acc_ref[a, 2 * band : 2 * band + 2].reshape(16, 128)
            out_ref[band, a * 16 : a * 16 + 16, :] = piece.astype(BF16)


def sum_kernel(in_ref, out_ref):
    lane = lax.broadcasted_iota(jnp.int32, (16, 128), 1) // 32
    masks = [lane == a for a in range(4)]
    for core in range(2):
        for h in range(2):
            parts = []
            for a in range(4):
                at = (h * 4 + a) * 16
                total = in_ref[core, at : at + 16, :].astype(F32)
                for z in range(1, 8):
                    total = total + in_ref[2 * z + core, at : at + 16, :].astype(F32)
                parts.append(total)
            for g in range(4):
                row = jnp.zeros((16, 128), F32)
                for a in range(4):
                    shift = (32 * (a - g)) % 128
                    moved = pltpu.roll(parts[a], shift, 1) if shift else parts[a]
                    row = jnp.where(masks[a], moved, row)
                out_ref[0, (g // 2) * 4 + 2 * core + g % 2, :, 128 * h : 128 * h + 128] = row


VM = pl.BlockSpec(memory_space=pltpu.VMEM)
SM = pl.BlockSpec(memory_space=pltpu.SMEM)
HBM = pl.BlockSpec(memory_space=pltpu.HBM)
call = functools.partial(
    pl.pallas_call, compiler_params=pltpu.CompilerParams(vmem_limit_bytes=16 << 20)
)


def pinned(x):
    return pltpu.with_memory_space_constraint(x, pltpu.HBM)


def pack(*args):
    return call(
        pack_kernel,
        out_shape=(
            jax.ShapeDtypeStruct((PEERS, 24, 256), BF16),
            jax.ShapeDtypeStruct((8, 32, 16, 128), BF16),
        ),
        in_specs=[HBM] * 7,
        out_specs=(VM, HBM),
        scratch_shapes=[pltpu.SMEM(args[0].shape, jnp.int32)]
        + [pltpu.VMEM(a.shape, a.dtype) for a in args[1:]]
        + [
            pltpu.VMEM((32, 256), F32),
            pltpu.VMEM((512, 128), F32),
            pltpu.VMEM((32, 16, 128), BF16),
            pltpu.SMEM((SLOTS,), jnp.int32),
            pltpu.SMEM((PEERS,), jnp.int32),
            pltpu.SemaphoreType.DMA((8,)),
        ],
        name="pack",
    )(*[pinned(a) for a in args])


def images(recv, sibling, freq):
    xrow = np.broadcast_to(((ROW_L - 16.0) / SUB)[:, None], (SUB, 256)).astype(np.float32)
    ycol = np.broadcast_to(((np.arange(16) + 0.5) / SUB)[:, None], (16, 256)).astype(np.float32)
    args = (freq, jnp.asarray(spread_tables(), BF16), jnp.asarray(xrow), jnp.asarray(ycol))
    return call(
        image_kernel,
        out_shape=(
            jax.ShapeDtypeStruct((2 * SLOTS, SUB, 128), F32),
            jax.ShapeDtypeStruct((8, 512), jnp.int32),
        ),
        in_specs=[VM, VM] + [HBM] * 4,
        out_specs=(VM, HBM),
        scratch_shapes=[pltpu.VMEM(a.shape, a.dtype) for a in args]
        + [pltpu.VMEM((8, 512), jnp.int32)]
        + [pltpu.VMEM((2 * PEERS, 8, 256), F32)] * 3
        + [pltpu.SemaphoreType.DMA((5,))],
        name="images",
    )(recv, sibling, *[pinned(a) for a in args])


def grid_tile(ints, image, own, other):
    tables = (
        jnp.asarray(taper_table()),
        jnp.asarray(replicate_tables(), BF16),
        jnp.asarray(column_table(), BF16),
        jnp.asarray(row_table(), BF16),
    )
    return call(
        grid_kernel,
        out_shape=jax.ShapeDtypeStruct((16, 128, 128), BF16),
        in_specs=[HBM, VM, VM, VM] + [HBM] * 4,
        out_specs=VM,
        scratch_shapes=[pltpu.SMEM(ints.shape, jnp.int32)]
        + [pltpu.VMEM(t.shape, t.dtype) for t in tables]
        + [pltpu.VMEM((9, 33, 8, 128), F32), pltpu.SemaphoreType.DMA((5,))],
        name="grid_tile",
    )(pinned(ints), image, own, other, *[pinned(t) for t in tables])


def band_sum(arrived):
    return call(
        sum_kernel,
        out_shape=jax.ShapeDtypeStruct((1, 8, 16, 256), F32),
        in_specs=[VM],
        out_specs=VM,
        name="band_sum",
    )(arrived)


SWAP = [(0, 1), (1, 0)]


def on_device(visibilities, weights, uv_coords, freq_ratio, screens, stations, offsets, tile_ids):
    uv = jnp.transpose(uv_coords, (1, 2, 0)).reshape(32, 32)
    pairs = jnp.transpose(screens.reshape(32, 2, 8, 128), (0, 2, 1, 3)).reshape(32, 16, 128)
    packed, mine = pack(tile_ids.T, visibilities, weights, uv, stations.T, offsets.T, pairs)
    recv = lax.all_to_all(packed, "tile", split_axis=0, concat_axis=0, tiled=True)
    own = lax.all_to_all(mine, "z", split_axis=0, concat_axis=0, tiled=True).reshape(256, 16, 128)
    sibling = lax.ppermute(recv, "core", SWAP)
    image, ints = images(recv.reshape(96, 8, 256), sibling.reshape(96, 8, 256), freq_ratio[None, :])
    own, image = lax.optimization_barrier((own, image))
    other = lax.ppermute(own, "core", SWAP)
    partial = grid_tile(ints, image, own, other)
    arrived = lax.all_to_all(partial, ("z", "core"), split_axis=0, concat_axis=0, tiled=True)
    return band_sum(arrived)


def solution(mesh):
    stat, tile = mesh.shape["stat"], mesh.shape["tile"]
    fine = Mesh(mesh.devices.reshape(stat // 2, 2, tile), ("z", "core", "tile"))
    every = ("z", "core", "tile")
    placed = (
        P(every, None, None),
        P(every, None),
        P(every, None, None),
        P(),
        P(("z", "core"), None, None),
        P(every, None),
        P(every, None),
        P(every, None),
    )
    return jax.shard_map(
        on_device,
        mesh=fine,
        in_specs=placed,
        out_specs=P("tile", None, ("z", "core"), None),
        check_vma=False,
    )
```

time: 99.7 us -> 95.4 us (0.957)
  blocking collectives: 20.4 us -> 42.1 us
  waiting for transfers between devices: 26.7 us -> 9.76 us
  starting transfers between devices: 28.8 us -> 22 us
  local copies, waits for them, and re-layouts: 2.69 us -> 0.6 us
    all_to_all x1 -> x2, blocking collectives: 20.4 us -> 42.1 us  [the longest x1 21.9 us: on_device(): lax.all_to_all(packed, 'tile', split_axis=0, concat_axis=0, tiled=True)]
    all_to_all x1 -> x0, waiting for transfers between devices: 10.6 us -> none  [on_device(): lax.all_to_all(packed, 'tile', split_axis=0, concat_axis=0, tiled=True)]
    all_to_all x1 -> x0, starting transfers between devices: 10.5 us -> none  [on_device(): lax.all_to_all(packed, 'tile', split_axis=0, concat_axis=0, tiled=True)]
    all_to_all x1, waiting for transfers between devices: 12.2 us -> 6.17 us  [on_device(): lax.all_to_all(mine, 'z', split_axis=0, concat_axis=0, tiled=True)]
    ppermute x1, starting transfers between devices: 2.27 us -> 6.01 us  [on_device(): sibling = lax.ppermute(recv, 'core', SWAP)]
    broadcast_in_dim x2 -> x0, local copies, waits for them, and re-layouts: 2.1 us -> none  [on_device(): mine = jnp.broadcast_to(screens.reshape(1, 32, 16, 128), (8, 32, 16, 128))]
  transfers between devices with their start and end apart: 4 -> 3, of which waited for: 4 -> 3; matrix products, arithmetic and copies ran while one was open for 1% -> 0% of each run, Pallas kernels for 13% -> 12%
where the time goes in v2:
time: 95.4 us; the launch traced here: 94 us
  blocking collectives  42.1 us (44%)
  starting transfers between devices  22 us (23%)
  Pallas kernels  19.4 us (20%)
  waiting for transfers between devices  9.76 us (10%)
    all_to_all x1, blocking collectives, on_device(): lax.all_to_all(packed, 'tile', split_axis=0, concat_axis=0, tiled=True)  21.9 us
    all_to_all x1, blocking collectives, on_device(): lax.all_to_all(partial, ('z', 'core'), split_axis=0, concat_axis=0, tiled...  20.2 us
    pallas_call x1, Pallas kernels, images(): call(image_kernel, out_shape=(jax.ShapeDtypeStruct((2 * SLOTS, SUB, 128),...  11.5 us
    all_to_all x1, starting transfers between devices, on_device(): lax.all_to_all(mine, 'z', split_axis=0, concat_axis=0, tiled=True)  10 us
    all_to_all x1, waiting for transfers between devices, on_device(): lax.all_to_all(mine, 'z', split_axis=0, concat_axis=0, tiled=True)  6.17 us
    ppermute x1, starting transfers between devices, on_device(): sibling = lax.ppermute(recv, 'core', SWAP)  6.01 us
    ppermute x1, starting transfers between devices, on_device(): other = lax.ppermute(own, 'core', SWAP)  5.99 us
    pallas_call x1, Pallas kernels, grid_tile(): call(grid_kernel, out_shape=jax.ShapeDtypeStruct((16, 128, 128), BF16), i...  4.63 us
  transfers between devices with their start and end apart: 3, of which 3 were waited for; matrix products, arithmetic and copies ran while one was open for 0% of the time, Pallas kernels for 12%

profile of v2, /device:TPU:1, one launch (start us, length us, event | category | flops | bytes accessed | tf_op | source)
XLA Modules:
  0.0 94.0 jit_solution(10097316601536576552)
XLA Ops:
  0.0 2.4 %pack.1 = (bf16[32,24,256]{2,1,0:T(8,128)(2,1)S(1)}, bf16[8,32,16,128]{3,2,1,0:T(8,128)(2,1)}) custom-call(s32[1,32]{1,0:T(1,128)} %bitcast.24, f32[32,8,256]{2,1,0:T(8,128)} %vis_in.1, f32[32,256]{1,0:T(8,128)} %weight_in.1, f32[32,32]{1,0:T(8,128)} %bitcast.20, s32[2,32]{1,0:T(2,128)} %bitcast.21, s32[2,32]{1,0:T(2,128)} %bitcast.22, ...), custom_call_target="tpu_custom_call" | custom-call | tf_op jit(solution)/shard_map/pack/pallas_call | solution.py:355
  2.4 21.9 %all_to_all.15 = bf16[32,24,256]{2,1,0:T(8,128)(2,1)S(1)} all-to-all(bf16[32,24,256]{2,1,0:T(8,128)(2,1)S(1)} %get-tuple-element.11), channel_id=1, replica_groups=mesh['z'=8,'core'=2,'tile'=32] {'tile'}, dimensions={0} | all-to-all | bytes 786432 | tf_op jit(solution)/shard_map/all_to_all | solution.py:433
  24.4 10.0 %all-to-all-start.1 = ((bf16[8,32,16,128]{3,2,1,0:T(8,128)(2,1)}), bf16[8,32,16,128]{3,2,1,0:T(8,128)(2,1)S(1)}, u32[]{:S(2)}, u32[]{:S(2)}) async-start(bf16[8,32,16,128]{3,2,1,0:T(8,128)(2,1)} %get-tuple-element.13), calls=%async_computation.1 | async-start | bytes 2097152 | tf_op jit(solution)/shard_map/all_to_all | solution.py:434
  34.4 6.0 %collective-permute-start = (bf16[32,24,256]{2,1,0:T(8,128)(2,1)S(1)}, bf16[32,24,256]{2,1,0:T(8,128)(2,1)S(1)}, u32[]{:S(2)}, u32[]{:S(2)}) collective-permute-start(bf16[32,24,256]{2,1,0:T(8,128)(2,1)S(1)} %all_to_all.15), channel_id=1, source_target_pairs={{0,32},{32,0},{1,33},{33,1},{2,34},{34,2},{3,35},{35,3},{4,36},{36... | collective-permute-start | bytes 1179656 | tf_op jit(solution)/shard_map/ppermute | solution.py:435
  40.4 1.3 %collective-permute-done = bf16[32,24,256]{2,1,0:T(8,128)(2,1)S(1)} collective-permute-done((bf16[32,24,256]{2,1,0:T(8,128)(2,1)S(1)}, bf16[32,24,256]{2,1,0:T(8,128)(2,1)S(1)}, u32[]{:S(2)}, u32[]{:S(2)}) %collective-permute-start) | collective-permute-done | bytes 393248 | tf_op jit(solution)/shard_map/ppermute | solution.py:435
  41.8 11.5 %images.1 = (f32[128,32,128]{2,1,0:T(8,128)S(1)}, s32[8,512]{1,0:T(8,128)S(1)}) custom-call(bf16[96,8,256]{2,1,0:T(8,128)(2,1)S(1)} %bitcast.17, bf16[96,8,256]{2,1,0:T(8,128)(2,1)S(1)} %bitcast.18, f32[1,16]{1,0:T(1,128)} %bitcast.23, bf16[4,256,256]{2,1,0:T(8,128)(2,1)} %constant.14.clone.spread_in, f32[32,256]{1,0:T(8,128)} %constant.15.clone.xrow_in, ...), custom_call_target="tpu_custom_call" | custom-call | tf_op jit(solution)/shard_map/images/pallas_call | solution.py:381
  53.3 0.0 copy-start
  53.3 0.6 copy-done
  53.9 6.2 %all-to-all-done.1 = bf16[8,32,16,128]{3,2,1,0:T(8,128)(2,1)S(1)} async-done(((bf16[8,32,16,128]{3,2,1,0:T(8,128)(2,1)}), bf16[8,32,16,128]{3,2,1,0:T(8,128)(2,1)S(1)}, u32[]{:S(2)}, u32[]{:S(2)}) %all-to-all-start.1) | async-done | bytes 1048608 | tf_op jit(solution)/shard_map/all_to_all | solution.py:434
  60.1 6.0 %collective-permute-start.1 = (bf16[256,16,128]{2,1,0:T(8,128)(2,1)S(1)}, bf16[256,16,128]{2,1,0:T(8,128)(2,1)S(1)}, u32[]{:S(2)}, u32[]{:S(2)}) collective-permute-start(bf16[256,16,128]{2,1,0:T(8,128)(2,1)S(1)} %bitcast.15), channel_id=1, source_target_pairs={{0,32},{32,0},{1,33},{33,1},{2,34},{34,2},{3,35},{35,3},{4,36},{36... | collective-permute-start | bytes 3145736 | tf_op jit(solution)/shard_map/ppermute | solution.py:438
  66.1 2.3 %collective-permute-done.1.other_ref = bf16[256,16,128]{2,1,0:T(8,128)(2,1)S(1)} collective-permute-done((bf16[256,16,128]{2,1,0:T(8,128)(2,1)S(1)}, bf16[256,16,128]{2,1,0:T(8,128)(2,1)S(1)}, u32[]{:S(2)}, u32[]{:S(2)}) %collective-permute-start.1) | collective-permute-done | bytes 1048608 | tf_op jit(solution)/shard_map/ppermute | solution.py:438
  68.3 4.6 %grid_tile.1 = bf16[16,128,128]{2,1,0:T(8,128)(2,1)S(1)} custom-call(s32[8,512]{1,0:T(8,128)} %copy-done, f32[128,32,128]{2,1,0:T(8,128)S(1)} %get-tuple-element.15.i_ref, bf16[256,16,128]{2,1,0:T(8,128)(2,1)S(1)} %bitcast.16, bf16[256,16,128]{2,1,0:T(8,128)(2,1)S(1)} %collective-permute-done.1.other_ref, f32[8,128]{1,0:T(8,128)} %constant.17.clone.taper_in, ...), custom_call_target="tpu_custom_call" | custom-call | tf_op jit(solution)/shard_map/grid_tile/pallas_call | solution.py:404
  73.0 20.2 %all_to_all.16.in_ref = bf16[16,128,128]{2,1,0:T(8,128)(2,1)S(1)} all-to-all(bf16[16,128,128]{2,1,0:T(8,128)(2,1)S(1)} %grid_tile.1), channel_id=1, replica_groups=mesh['z'=8,'core'=2,'tile'=32] {'z','core'}, dimensions={0} | all-to-all | bytes 1048576 | tf_op jit(solution)/shard_map/all_to_all | solution.py:440
  93.1 0.8 band_sum.1
Async XLA Ops:
  24.4 35.7 %all-to-all-start.1 = ((bf16[8,32,16,128]{3,2,1,0:T(8,128)(2,1)}), bf16[8,32,16,128]{3,2,1,0:T(8,128)(2,1)S(1)}, u32[]{:S(2)}, u32[]{:S(2)}) async-start(bf16[8,32,16,128]{3,2,1,0:T(8,128)(2,1)} %get-tuple-element.13), calls=%async_computation.1 | async-start | bytes 2097152 | tf_op jit(solution)/shard_map/all_to_all | solution.py:434
  34.4 7.3 %collective-permute-start = (bf16[32,24,256]{2,1,0:T(8,128)(2,1)S(1)}, bf16[32,24,256]{2,1,0:T(8,128)(2,1)S(1)}, u32[]{:S(2)}, u32[]{:S(2)}) collective-permute-start(bf16[32,24,256]{2,1,0:T(8,128)(2,1)S(1)} %all_to_all.15), channel_id=1, source_target_pairs={{0,32},{32,0},{1,33},{33,1},{2,34},{34,2},{3,35},{35,3},{4,36},{36... | collective-permute-start | bytes 1179656 | tf_op jit(solution)/shard_map/ppermute | solution.py:435
  53.3 0.6 copy-start
  60.1 8.3 %collective-permute-start.1 = (bf16[256,16,128]{2,1,0:T(8,128)(2,1)S(1)}, bf16[256,16,128]{2,1,0:T(8,128)(2,1)S(1)}, u32[]{:S(2)}, u32[]{:S(2)}) collective-permute-start(bf16[256,16,128]{2,1,0:T(8,128)(2,1)S(1)} %bitcast.15), channel_id=1, source_target_pairs={{0,32},{32,0},{1,33},{33,1},{2,34},{34,2},{3,35},{35,3},{4,36},{36... | collective-permute-start | bytes 3145736 | tf_op jit(solution)/shard_map/ppermute | solution.py:438

commit v3 on v2

--- a/solution.py
+++ b/solution.py
@@ -98,13 +98,13 @@
 
 
 def pack_kernel(
-    tile_in, vis_in, weight_in, uv_in, station_in, offset_in, screen_in, out_ref, mine_out,
+    tile_in, vis_in, weight_in, uv_in, station_in, offset_in, screen_in, out_ref, mine_ref,
     tile_ref, vis_ref, weight_ref, uv_ref, station_ref, offset_ref, screen_ref,
-    meta_ref, wide_ref, mine_ref, src_ref, count_ref, sem,
+    meta_ref, wide_ref, src_ref, count_ref, sem,
 ):
     pairs = (
         (tile_in, tile_ref), (station_in, station_ref), (offset_in, offset_ref),
-        (uv_in, uv_ref), (weight_in, weight_ref), (vis_in, vis_ref), (screen_in, screen_ref),
+        (uv_in, uv_ref), (weight_in, weight_ref), (vis_in, vis_ref), (screen_in.at[pl.ds(8 * lax.axis_index("x"), 8)], screen_ref),
     )
     copies = fetch(pairs, sem)
     for copy in copies[:4]:
@@ -162,10 +162,14 @@
 
     lax.fori_loop(0, PEERS, one_peer, 0, unroll=4)
     copies[6].wait()
-    wide_ref[...] = screen_ref[...].astype(F32).reshape(512, 128)
-    parts = [wide_ref[pl.ds(ri, 256, stride=2), :].reshape(32, 8, 128) for ri in range(2)]
+    wide_ref[...] = screen_ref[...].astype(F32).reshape(128, 128)
+    parts = [wide_ref[pl.ds(ri, 64, stride=2), :].reshape(8, 8, 128) for ri in range(2)]
     mine_ref[...] = jnp.concatenate(parts, axis=1).astype(BF16)
-    sends = fetch([(mine_ref, mine_out.at[z]) for z in range(8)], sem)
+
+
+def collect_kernel(in_ref, out_ref, sem):
+    core = lax.axis_index("core")
+    sends = fetch([(in_ref.at[:, core], out_ref.at[x]) for x in range(4)], sem)
     for send in sends:
         send.wait()
 
@@ -258,7 +262,7 @@
     group_mask = [(lane16 == 2 * a + upper).astype(F32).astype(BF16) for a in range(2)]
 
     def station(z_core, at):
-        where = (z_core >> 1) * 32 + at
+        where = ((at >> 3) * 8 + (z_core >> 1)) * 8 + (at & 7)
         mine = (z_core & 1) == core
         return jnp.where(mine, own_ref[where], other_ref[where]).astype(F32)
 
@@ -356,22 +360,33 @@
         pack_kernel,
         out_shape=(
             jax.ShapeDtypeStruct((PEERS, 24, 256), BF16),
-            jax.ShapeDtypeStruct((8, 32, 16, 128), BF16),
+            jax.ShapeDtypeStruct((8, 16, 128), BF16),
         ),
         in_specs=[HBM] * 7,
-        out_specs=(VM, HBM),
+        out_specs=(VM, VM),
         scratch_shapes=[pltpu.SMEM(args[0].shape, jnp.int32)]
-        + [pltpu.VMEM(a.shape, a.dtype) for a in args[1:]]
+        + [pltpu.VMEM(a.shape, a.dtype) for a in args[1:6]]
         + [
+            pltpu.VMEM((8, 16, 128), BF16),
             pltpu.VMEM((32, 256), F32),
-            pltpu.VMEM((512, 128), F32),
-            pltpu.VMEM((32, 16, 128), BF16),
+            pltpu.VMEM((128, 128), F32),
             pltpu.SMEM((SLOTS,), jnp.int32),
             pltpu.SMEM((PEERS,), jnp.int32),
             pltpu.SemaphoreType.DMA((8,)),
         ],
         name="pack",
     )(*[pinned(a) for a in args])
+
+
+def collect(quarter):
+    return call(
+        collect_kernel,
+        out_shape=jax.ShapeDtypeStruct((4, 8, 8, 16, 128), BF16),
+        in_specs=[VM],
+        out_specs=HBM,
+        scratch_shapes=[pltpu.SemaphoreType.DMA((4,))],
+        name="collect",
+    )(quarter)
 
 
 def images(recv, sibling, freq):
@@ -430,8 +445,9 @@
     uv = jnp.transpose(uv_coords, (1, 2, 0)).reshape(32, 32)
     pairs = jnp.transpose(screens.reshape(32, 2, 8, 128), (0, 2, 1, 3)).reshape(32, 16, 128)
     packed, mine = pack(tile_ids.T, visibilities, weights, uv, stations.T, offsets.T, pairs)
-    recv = lax.all_to_all(packed, "tile", split_axis=0, concat_axis=0, tiled=True)
-    own = lax.all_to_all(mine, "z", split_axis=0, concat_axis=0, tiled=True).reshape(256, 16, 128)
+    recv = lax.all_to_all(packed, ("x", "y"), split_axis=0, concat_axis=0, tiled=True)
+    quarter = lax.all_gather(mine, ("z", "core"), axis=0, tiled=True).reshape(8, 2, 8, 16, 128)
+    own = lax.all_to_all(collect(quarter), "x", split_axis=0, concat_axis=0, tiled=True).reshape(256, 16, 128)
     sibling = lax.ppermute(recv, "core", SWAP)
     image, ints = images(recv.reshape(96, 8, 256), sibling.reshape(96, 8, 256), freq_ratio[None, :])
     own, image = lax.optimization_barrier((own, image))
@@ -443,8 +459,8 @@
 
 def solution(mesh):
     stat, tile = mesh.shape["stat"], mesh.shape["tile"]
-    fine = Mesh(mesh.devices.reshape(stat // 2, 2, tile), ("z", "core", "tile"))
-    every = ("z", "core", "tile")
+    every = ("z", "core", "x", "y")
+    fine = Mesh(mesh.devices.reshape(stat // 2, 2, 4, tile // 4), every)
     placed = (
         P(every, None, None),
         P(every, None),
@@ -459,6 +475,6 @@
         on_device,
         mesh=fine,
         in_specs=placed,
-        out_specs=P("tile", None, ("z", "core"), None),
+        out_specs=P(("x", "y"), None, ("z", "core"), None),
         check_vma=False,
     )

time: 95.4 us -> 90.3 us (0.947)
  waiting for transfers between devices: 9.76 us -> 3.61 us
  blocking collectives: 42.1 us -> 45.6 us
  starting transfers between devices: 22 us -> 19.4 us
  Pallas kernels: 19.4 us -> 20.5 us
    all_gather x0 -> x1, blocking collectives: none -> 25.4 us  [on_device(): lax.all_gather(mine, ('z', 'core'), axis=0, tiled=True)]
    all_to_all x1 -> x0, blocking collectives: 21.9 us -> none  [on_device(): lax.all_to_all(packed, 'tile', split_axis=0, concat_axis=0, tiled=True)]
    all_to_all x1 -> x2, waiting for transfers between devices: 6.17 us -> 0.01 us  [the longest x1 0.01 us: on_device(): lax.all_to_all(packed, ('x', 'y'), split_axis=0, concat_axis=0, tiled=True)]
    all_to_all x1 -> x2, starting transfers between devices: 10 us -> 14.8 us  [the longest x1 10.5 us: on_device(): lax.all_to_all(packed, ('x', 'y'), split_axis=0, concat_axis=0, tiled=True)]
    ppermute x1, starting transfers between devices: 5.99 us -> 2.26 us  [on_device(): other = lax.ppermute(own, 'core', SWAP)]
    ppermute x1, starting transfers between devices: 6.01 us -> 2.34 us  [on_device(): sibling = lax.ppermute(recv, 'core', SWAP)]
    pallas_call x0 -> x1, Pallas kernels: none -> 1 us  [collect(): call(collect_kernel, out_shape=jax.ShapeDtypeStruct((4, 8, 8, 16, 128), B...]
  transfers between devices with their start and end apart: 3 -> 4, of which waited for: 3 -> 2; matrix products, arithmetic and copies ran while one was open for 0% -> 0% of each run, Pallas kernels for 12% -> 14%
where the time goes in v3:
time: 90.3 us; the launch traced here: 89.8 us
  blocking collectives  45.6 us (50%)
  Pallas kernels  20.5 us (23%)
  starting transfers between devices  19.4 us (21%)
  waiting for transfers between devices  3.61 us (4%)
    all_gather x1, blocking collectives, on_device(): lax.all_gather(mine, ('z', 'core'), axis=0, tiled=True)  25.4 us
    all_to_all x1, blocking collectives, on_device(): lax.all_to_all(partial, ('z', 'core'), split_axis=0, concat_axis=0, tiled...  20.2 us
    pallas_call x1, Pallas kernels, images(): call(image_kernel, out_shape=(jax.ShapeDtypeStruct((2 * SLOTS, SUB, 128),...  11.5 us
    all_to_all x1, starting transfers between devices, on_device(): lax.all_to_all(packed, ('x', 'y'), split_axis=0, concat_axis=0, tiled=True)  10.5 us
    pallas_call x1, Pallas kernels, grid_tile(): call(grid_kernel, out_shape=jax.ShapeDtypeStruct((16, 128, 128), BF16), i...  4.97 us
    all_to_all x1, starting transfers between devices, on_device(): lax.all_to_all(collect(quarter), 'x', split_axis=0, concat_axis=0, tiled=...  4.3 us
    ppermute x1, starting transfers between devices, on_device(): sibling = lax.ppermute(recv, 'core', SWAP)  2.34 us
    ppermute x1, waiting for transfers between devices, on_device(): other = lax.ppermute(own, 'core', SWAP)  2.27 us
  transfers between devices with their start and end apart: 4, of which 2 were waited for; matrix products, arithmetic and copies ran while one was open for 0% of the time, Pallas kernels for 14%

profile of v3, /device:TPU:1, one launch (start us, length us, event | category | flops | bytes accessed | tf_op | source)
XLA Modules:
  0.0 89.8 jit_solution(2917400913964387136)
XLA Ops:
  0.0 2.2 %pack.1 = (bf16[32,24,256]{2,1,0:T(8,128)(2,1)}, bf16[8,16,128]{2,1,0:T(8,128)(2,1)S(1)}) custom-call(s32[1,32]{1,0:T(1,128)} %bitcast.26, f32[32,8,256]{2,1,0:T(8,128)} %vis_in.1, f32[32,256]{1,0:T(8,128)} %weight_in.1, f32[32,32]{1,0:T(8,128)} %bitcast.22, s32[2,32]{1,0:T(2,128)} %bitcast.23, s32[2,32]{1,0:T(2,128)} %bitcast.24, bf16[32,16,128]{2,1,0:T(8,128)(2,1)} %bitcast.21), custom_call_target="tpu_custom_call" | custom-call | tf_op jit(solution)/shard_map/pack/pallas_call | solution.py:359
  2.2 10.5 %all-to-all-start = ((bf16[32,24,256]{2,1,0:T(8,128)(2,1)}), bf16[32,24,256]{2,1,0:T(8,128)(2,1)S(1)}, u32[]{:S(2)}, u32[]{:S(2)}) async-start(bf16[32,24,256]{2,1,0:T(8,128)(2,1)} %get-tuple-element.11), calls=%async_computation | async-start | bytes 786432 | tf_op jit(solution)/shard_map/all_to_all | solution.py:448
  12.7 25.4 %all_gather.3 = bf16[128,16,128]{2,1,0:T(8,128)(2,1)S(1)} all-gather(bf16[8,16,128]{2,1,0:T(8,128)(2,1)S(1)} %get-tuple-element.13), channel_id=1, replica_groups=mesh['z'=8,'core'=2,'x'=4,'y'=8] {'z','core'}, dimensions={0}, use_global_device_ids=true | all-gather | bytes 557056 | tf_op jit(solution)/shard_map/all_gather | solution.py:449
  38.1 1.0 %collect.1 = bf16[4,8,8,16,128]{4,3,2,1,0:T(8,128)(2,1)} custom-call(bf16[8,2,8,16,128]{4,3,2,1,0:T(8,128)(2,1)S(1)} %bitcast.18), custom_call_target="tpu_custom_call" | custom-call | tf_op jit(solution)/shard_map/collect/pallas_call | solution.py:382
  39.1 0.0 all-to-all-done
  39.1 4.3 %all-to-all-start.1 = ((bf16[4,8,8,16,128]{4,3,2,1,0:T(8,128)(2,1)}), bf16[4,8,8,16,128]{4,3,2,1,0:T(8,128)(2,1)S(1)}, u32[]{:S(2)}, u32[]{:S(2)}) async-start(bf16[4,8,8,16,128]{4,3,2,1,0:T(8,128)(2,1)} %collect.1), calls=%async_computation.1 | async-start | bytes 2097152 | tf_op jit(solution)/shard_map/all_to_all | solution.py:450
  43.4 2.3 %collective-permute-start = (bf16[32,24,256]{2,1,0:T(8,128)(2,1)S(1)}, bf16[32,24,256]{2,1,0:T(8,128)(2,1)S(1)}, u32[]{:S(2)}, u32[]{:S(2)}) collective-permute-start(bf16[32,24,256]{2,1,0:T(8,128)(2,1)S(1)} %all-to-all-done), channel_id=1, source_target_pairs={{0,32},{32,0},{1,33},{33,1},{2,34},{34,2},{3,35},{35,3},{4,36},{36... | collective-permute-start | bytes 1179656 | tf_op jit(solution)/shard_map/ppermute | solution.py:451
  45.8 1.3 %collective-permute-done = bf16[32,24,256]{2,1,0:T(8,128)(2,1)S(1)} collective-permute-done((bf16[32,24,256]{2,1,0:T(8,128)(2,1)S(1)}, bf16[32,24,256]{2,1,0:T(8,128)(2,1)S(1)}, u32[]{:S(2)}, u32[]{:S(2)}) %collective-permute-start) | collective-permute-done | bytes 393248 | tf_op jit(solution)/shard_map/ppermute | solution.py:451
  47.1 11.5 %images.1 = (f32[128,32,128]{2,1,0:T(8,128)S(1)}, s32[8,512]{1,0:T(8,128)S(1)}) custom-call(bf16[96,8,256]{2,1,0:T(8,128)(2,1)S(1)} %bitcast.19, bf16[96,8,256]{2,1,0:T(8,128)(2,1)S(1)} %bitcast.20, f32[1,16]{1,0:T(1,128)} %bitcast.25, bf16[4,256,256]{2,1,0:T(8,128)(2,1)} %constant.14.clone.spread_in, f32[32,256]{1,0:T(8,128)} %constant.15.clone.xrow_in, ...), custom_call_target="tpu_custom_call" | custom-call | tf_op jit(solution)/shard_map/images/pallas_call | solution.py:396
  58.6 0.0 copy-start
  58.6 0.6 copy-done
  59.2 0.0 all-to-all-done.1
  59.2 2.3 %collective-permute-start.1 = (bf16[256,16,128]{2,1,0:T(8,128)(2,1)S(1)}, bf16[256,16,128]{2,1,0:T(8,128)(2,1)S(1)}, u32[]{:S(2)}, u32[]{:S(2)}) collective-permute-start(bf16[256,16,128]{2,1,0:T(8,128)(2,1)S(1)} %bitcast.16), channel_id=1, source_target_pairs={{0,32},{32,0},{1,33},{33,1},{2,34},{34,2},{3,35},{35,3},{4,36},{36... | collective-permute-start | bytes 3145736 | tf_op jit(solution)/shard_map/ppermute | solution.py:454
  61.5 2.3 %collective-permute-done.1.other_ref = bf16[256,16,128]{2,1,0:T(8,128)(2,1)S(1)} collective-permute-done((bf16[256,16,128]{2,1,0:T(8,128)(2,1)S(1)}, bf16[256,16,128]{2,1,0:T(8,128)(2,1)S(1)}, u32[]{:S(2)}, u32[]{:S(2)}) %collective-permute-start.1) | collective-permute-done | bytes 1048608 | tf_op jit(solution)/shard_map/ppermute | solution.py:454
  63.8 5.0 %grid_tile.1 = bf16[16,128,128]{2,1,0:T(8,128)(2,1)S(1)} custom-call(s32[8,512]{1,0:T(8,128)} %copy-done, f32[128,32,128]{2,1,0:T(8,128)S(1)} %get-tuple-element.15.i_ref, bf16[256,16,128]{2,1,0:T(8,128)(2,1)S(1)} %bitcast.17, bf16[256,16,128]{2,1,0:T(8,128)(2,1)S(1)} %collective-permute-done.1.other_ref, f32[8,128]{1,0:T(8,128)} %constant.17.clone.taper_in, ...), custom_call_target="tpu_custom_call" | custom-call | tf_op jit(solution)/shard_map/grid_tile/pallas_call | solution.py:419
  68.8 20.2 %all_to_all.15.in_ref = bf16[16,128,128]{2,1,0:T(8,128)(2,1)S(1)} all-to-all(bf16[16,128,128]{2,1,0:T(8,128)(2,1)S(1)} %grid_tile.1), channel_id=1, replica_groups=mesh['z'=8,'core'=2,'x'=4,'y'=8] {'z','core'}, dimensions={0} | all-to-all | bytes 1048576 | tf_op jit(solution)/shard_map/all_to_all | solution.py:456
  89.0 0.8 band_sum.1
Async XLA Ops:
  2.2 36.9 %all-to-all-start = ((bf16[32,24,256]{2,1,0:T(8,128)(2,1)}), bf16[32,24,256]{2,1,0:T(8,128)(2,1)S(1)}, u32[]{:S(2)}, u32[]{:S(2)}) async-start(bf16[32,24,256]{2,1,0:T(8,128)(2,1)} %get-tuple-element.11), calls=%async_computation | async-start | bytes 786432 | tf_op jit(solution)/shard_map/all_to_all | solution.py:448
  39.1 20.1 %all-to-all-start.1 = ((bf16[4,8,8,16,128]{4,3,2,1,0:T(8,128)(2,1)}), bf16[4,8,8,16,128]{4,3,2,1,0:T(8,128)(2,1)S(1)}, u32[]{:S(2)}, u32[]{:S(2)}) async-start(bf16[4,8,8,16,128]{4,3,2,1,0:T(8,128)(2,1)} %collect.1), calls=%async_computation.1 | async-start | bytes 2097152 | tf_op jit(solution)/shard_map/all_to_all | solution.py:450
  43.4 3.7 %collective-permute-start = (bf16[32,24,256]{2,1,0:T(8,128)(2,1)S(1)}, bf16[32,24,256]{2,1,0:T(8,128)(2,1)S(1)}, u32[]{:S(2)}, u32[]{:S(2)}) collective-permute-start(bf16[32,24,256]{2,1,0:T(8,128)(2,1)S(1)} %all-to-all-done), channel_id=1, source_target_pairs={{0,32},{32,0},{1,33},{33,1},{2,34},{34,2},{3,35},{35,3},{4,36},{36... | collective-permute-start | bytes 1179656 | tf_op jit(solution)/shard_map/ppermute | solution.py:451
  58.6 0.6 copy-start
  59.2 4.5 %collective-permute-start.1 = (bf16[256,16,128]{2,1,0:T(8,128)(2,1)S(1)}, bf16[256,16,128]{2,1,0:T(8,128)(2,1)S(1)}, u32[]{:S(2)}, u32[]{:S(2)}) collective-permute-start(bf16[256,16,128]{2,1,0:T(8,128)(2,1)S(1)} %bitcast.16), channel_id=1, source_target_pairs={{0,32},{32,0},{1,33},{33,1},{2,34},{34,2},{3,35},{35,3},{4,36},{36... | collective-permute-start | bytes 3145736 | tf_op jit(solution)/shard_map/ppermute | solution.py:454

commit v4 on v3

--- a/solution.py
+++ b/solution.py
@@ -69,7 +69,7 @@
     s = (0.5 * np.cos(np.pi * (np.arange(400) + 0.5) / 800)) ** 2
     r = np.sqrt(s)
     cheb = np.polynomial.chebyshev.Chebyshev.fit
-    cos = cheb(s, np.cos(2 * np.pi * r), 6, domain=[0, 0.25]).convert(kind=np.polynomial.Polynomial)
+    cos = cheb(s, np.cos(2 * np.pi * r), 5, domain=[0, 0.25]).convert(kind=np.polynomial.Polynomial)
     sin = cheb(s, np.sin(2 * np.pi * r) / r, 5, domain=[0, 0.25]).convert(kind=np.polynomial.Polynomial)
     return [float(c) for c in cos.coef], [float(c) for c in sin.coef]
 
@@ -104,7 +104,7 @@
 ):
     pairs = (
         (tile_in, tile_ref), (station_in, station_ref), (offset_in, offset_ref),
-        (uv_in, uv_ref), (weight_in, weight_ref), (vis_in, vis_ref), (screen_in.at[pl.ds(8 * lax.axis_index("x"), 8)], screen_ref),
+        (uv_in, uv_ref), (weight_in, weight_ref), (vis_in, vis_ref), (screen_in.at[pl.ds(8 * (2 * lax.axis_index("xl") + lax.axis_index("yl")), 8)], screen_ref),
     )
     copies = fetch(pairs, sem)
     for copy in copies[:4]:
@@ -167,11 +167,12 @@
     mine_ref[...] = jnp.concatenate(parts, axis=1).astype(BF16)
 
 
-def collect_kernel(in_ref, out_ref, sem):
+def collect_kernel(in_ref, out_ref):
     core = lax.axis_index("core")
-    sends = fetch([(in_ref.at[:, core], out_ref.at[x]) for x in range(4)], sem)
-    for send in sends:
-        send.wait()
+    for z in range(8):
+        piece = in_ref[z, core]
+        for x in range(4):
+            out_ref[x, z] = piece
 
 
 def image_kernel(
@@ -234,11 +235,11 @@
                 one_slot(block_ref, b * PEERS + n, n, j, 4 * n + 2 * b + j)
         return c
 
-    lax.fori_loop(0, PEERS, one_peer, 0, unroll=2)
+    lax.fori_loop(0, PEERS, one_peer, 0, unroll=4)
     send.wait()
 
 
-GROUP = 32
+GROUP = 64
 
 
 def grid_kernel(
@@ -383,8 +384,7 @@
         collect_kernel,
         out_shape=jax.ShapeDtypeStruct((4, 8, 8, 16, 128), BF16),
         in_specs=[VM],
-        out_specs=HBM,
-        scratch_shapes=[pltpu.SemaphoreType.DMA((4,))],
+        out_specs=VM,
         name="collect",
     )(quarter)
 
@@ -445,9 +445,9 @@
     uv = jnp.transpose(uv_coords, (1, 2, 0)).reshape(32, 32)
     pairs = jnp.transpose(screens.reshape(32, 2, 8, 128), (0, 2, 1, 3)).reshape(32, 16, 128)
     packed, mine = pack(tile_ids.T, visibilities, weights, uv, stations.T, offsets.T, pairs)
-    recv = lax.all_to_all(packed, ("x", "y"), split_axis=0, concat_axis=0, tiled=True)
+    recv = lax.all_to_all(packed, ("xh", "xl", "yh", "yl"), split_axis=0, concat_axis=0, tiled=True)
     quarter = lax.all_gather(mine, ("z", "core"), axis=0, tiled=True).reshape(8, 2, 8, 16, 128)
-    own = lax.all_to_all(collect(quarter), "x", split_axis=0, concat_axis=0, tiled=True).reshape(256, 16, 128)
+    own = lax.all_to_all(collect(quarter), ("xl", "yl"), split_axis=0, concat_axis=0, tiled=True).reshape(256, 16, 128)
     sibling = lax.ppermute(recv, "core", SWAP)
     image, ints = images(recv.reshape(96, 8, 256), sibling.reshape(96, 8, 256), freq_ratio[None, :])
     own, image = lax.optimization_barrier((own, image))
@@ -459,8 +459,8 @@
 
 def solution(mesh):
     stat, tile = mesh.shape["stat"], mesh.shape["tile"]
-    every = ("z", "core", "x", "y")
-    fine = Mesh(mesh.devices.reshape(stat // 2, 2, 4, tile // 4), every)
+    every = ("z", "core", "xh", "xl", "yh", "yl")
+    fine = Mesh(mesh.devices.reshape(stat // 2, 2, 2, 2, tile // 8, 2), every)
     placed = (
         P(every, None, None),
         P(every, None),
@@ -475,6 +475,6 @@
         on_device,
         mesh=fine,
         in_specs=placed,
-        out_specs=P(("x", "y"), None, ("z", "core"), None),
+        out_specs=P(("xh", "xl", "yh", "yl"), None, ("z", "core"), None),
         check_vma=False,
     )

time: 90.3 us -> 88.1 us (0.976)
  Pallas kernels: 20.5 us -> 18.8 us
    pallas_call x1, Pallas kernels: 11.5 us -> 10.3 us  [images(): call(image_kernel, out_shape=(jax.ShapeDtypeStruct((2 * SLOTS, SUB, 128),...]
  transfers between devices with their start and end apart: 4 -> 4, of which waited for: 2 -> 2; matrix products, arithmetic and copies ran while one was open for 0% -> 0% of each run, Pallas kernels for 14% -> 13%
where the time goes in v4:
time: 88.1 us; the launch traced here: 87.5 us
  blocking collectives  45.6 us (52%)
  Pallas kernels  18.8 us (21%)
  starting transfers between devices  18.8 us (21%)
  waiting for transfers between devices  3.61 us (4%)
    all_gather x1, blocking collectives, on_device(): lax.all_gather(mine, ('z', 'core'), axis=0, tiled=True)  25.4 us
    all_to_all x1, blocking collectives, on_device(): lax.all_to_all(partial, ('z', 'core'), split_axis=0, concat_axis=0, tiled...  20.2 us
    all_to_all x1, starting transfers between devices, on_device(): lax.all_to_all(packed, ('xh', 'xl', 'yh', 'yl'), split_axis=0, concat_axi...  10.5 us
    pallas_call x1, Pallas kernels, images(): call(image_kernel, out_shape=(jax.ShapeDtypeStruct((2 * SLOTS, SUB, 128),...  10.3 us
    pallas_call x1, Pallas kernels, grid_tile(): call(grid_kernel, out_shape=jax.ShapeDtypeStruct((16, 128, 128), BF16), i...  4.42 us
    all_to_all x1, starting transfers between devices, on_device(): lax.all_to_all(collect(quarter), ('xl', 'yl'), split_axis=0, concat_axis=...  3.68 us
    ppermute x1, starting transfers between devices, on_device(): sibling = lax.ppermute(recv, 'core', SWAP)  2.34 us
    ppermute x1, waiting for transfers between devices, on_device(): other = lax.ppermute(own, 'core', SWAP)  2.27 us
  transfers between devices with their start and end apart: 4, of which 2 were waited for; matrix products, arithmetic and copies ran while one was open for 0% of the time, Pallas kernels for 13%

profile of v4, /device:TPU:1, one launch (start us, length us, event | category | flops | bytes accessed | tf_op | source)
XLA Modules:
  0.0 87.5 jit_solution(10050044265071897726)
XLA Ops:
  0.0 2.2 %pack.1 = (bf16[32,24,256]{2,1,0:T(8,128)(2,1)}, bf16[8,16,128]{2,1,0:T(8,128)(2,1)S(1)}) custom-call(s32[1,32]{1,0:T(1,128)} %bitcast.26, f32[32,8,256]{2,1,0:T(8,128)} %vis_in.1, f32[32,256]{1,0:T(8,128)} %weight_in.1, f32[32,32]{1,0:T(8,128)} %bitcast.22, s32[2,32]{1,0:T(2,128)} %bitcast.23, s32[2,32]{1,0:T(2,128)} %bitcast.24, bf16[32,16,128]{2,1,0:T(8,128)(2,1)} %bitcast.21), custom_call_target="tpu_custom_call" | custom-call | tf_op jit(solution)/shard_map/pack/pallas_call | solution.py:360
  2.2 10.5 %all-to-all-start = ((bf16[32,24,256]{2,1,0:T(8,128)(2,1)}), bf16[32,24,256]{2,1,0:T(8,128)(2,1)S(1)}, u32[]{:S(2)}, u32[]{:S(2)}) async-start(bf16[32,24,256]{2,1,0:T(8,128)(2,1)} %get-tuple-element.11), calls=%async_computation | async-start | bytes 786432 | tf_op jit(solution)/shard_map/all_to_all | solution.py:448
  12.7 25.4 %all_gather.3 = bf16[128,16,128]{2,1,0:T(8,128)(2,1)S(1)} all-gather(bf16[8,16,128]{2,1,0:T(8,128)(2,1)S(1)} %get-tuple-element.13), channel_id=1, replica_groups=mesh['z'=8,'core'=2,'xh'=2,'xl'=2,'yh'=4,'yl'=2] {'z','core'}, dimensions={0}, use_global_device_ids=true | all-gather | bytes 557056 | tf_op jit(solution)/shard_map/all_gather | solution.py:449
  38.1 1.1 %collect.1 = bf16[4,8,8,16,128]{4,3,2,1,0:T(8,128)(2,1)} custom-call(bf16[8,2,8,16,128]{4,3,2,1,0:T(8,128)(2,1)S(1)} %bitcast.18), custom_call_target="tpu_custom_call" | custom-call | tf_op jit(solution)/shard_map/collect/pallas_call | solution.py:383
  39.2 0.0 all-to-all-done
  39.2 3.7 %all-to-all-start.1 = ((bf16[4,8,8,16,128]{4,3,2,1,0:T(8,128)(2,1)}), bf16[4,8,8,16,128]{4,3,2,1,0:T(8,128)(2,1)S(1)}, u32[]{:S(2)}, u32[]{:S(2)}) async-start(bf16[4,8,8,16,128]{4,3,2,1,0:T(8,128)(2,1)} %collect.1), calls=%async_computation.1 | async-start | bytes 2097152 | tf_op jit(solution)/shard_map/all_to_all | solution.py:450
  42.9 2.3 %collective-permute-start = (bf16[32,24,256]{2,1,0:T(8,128)(2,1)S(1)}, bf16[32,24,256]{2,1,0:T(8,128)(2,1)S(1)}, u32[]{:S(2)}, u32[]{:S(2)}) collective-permute-start(bf16[32,24,256]{2,1,0:T(8,128)(2,1)S(1)} %all-to-all-done), channel_id=1, source_target_pairs={{0,32},{32,0},{1,33},{33,1},{2,34},{34,2},{3,35},{35,3},{4,36},{36... | collective-permute-start | bytes 1179656 | tf_op jit(solution)/shard_map/ppermute | solution.py:451
  45.2 1.3 %collective-permute-done = bf16[32,24,256]{2,1,0:T(8,128)(2,1)S(1)} collective-permute-done((bf16[32,24,256]{2,1,0:T(8,128)(2,1)S(1)}, bf16[32,24,256]{2,1,0:T(8,128)(2,1)S(1)}, u32[]{:S(2)}, u32[]{:S(2)}) %collective-permute-start) | collective-permute-done | bytes 393248 | tf_op jit(solution)/shard_map/ppermute | solution.py:451
  46.6 10.3 %images.1 = (f32[128,32,128]{2,1,0:T(8,128)S(1)}, s32[8,512]{1,0:T(8,128)S(1)}) custom-call(bf16[96,8,256]{2,1,0:T(8,128)(2,1)S(1)} %bitcast.19, bf16[96,8,256]{2,1,0:T(8,128)(2,1)S(1)} %bitcast.20, f32[1,16]{1,0:T(1,128)} %bitcast.25, bf16[4,256,256]{2,1,0:T(8,128)(2,1)} %constant.14.clone.spread_in, f32[32,256]{1,0:T(8,128)} %constant.15.clone.xrow_in, ...), custom_call_target="tpu_custom_call" | custom-call | tf_op jit(solution)/shard_map/images/pallas_call | solution.py:396
  56.9 0.0 copy-start
  56.9 0.6 copy-done
  57.5 0.0 all-to-all-done.1
  57.5 2.3 %collective-permute-start.1 = (bf16[256,16,128]{2,1,0:T(8,128)(2,1)S(1)}, bf16[256,16,128]{2,1,0:T(8,128)(2,1)S(1)}, u32[]{:S(2)}, u32[]{:S(2)}) collective-permute-start(bf16[256,16,128]{2,1,0:T(8,128)(2,1)S(1)} %bitcast.16), channel_id=1, source_target_pairs={{0,32},{32,0},{1,33},{33,1},{2,34},{34,2},{3,35},{35,3},{4,36},{36... | collective-permute-start | bytes 3145736 | tf_op jit(solution)/shard_map/ppermute | solution.py:454
  59.8 2.3 %collective-permute-done.1.other_ref = bf16[256,16,128]{2,1,0:T(8,128)(2,1)S(1)} collective-permute-done((bf16[256,16,128]{2,1,0:T(8,128)(2,1)S(1)}, bf16[256,16,128]{2,1,0:T(8,128)(2,1)S(1)}, u32[]{:S(2)}, u32[]{:S(2)}) %collective-permute-start.1) | collective-permute-done | bytes 1048608 | tf_op jit(solution)/shard_map/ppermute | solution.py:454
  62.0 4.4 %grid_tile.1 = bf16[16,128,128]{2,1,0:T(8,128)(2,1)S(1)} custom-call(s32[8,512]{1,0:T(8,128)} %copy-done, f32[128,32,128]{2,1,0:T(8,128)S(1)} %get-tuple-element.15.i_ref, bf16[256,16,128]{2,1,0:T(8,128)(2,1)S(1)} %bitcast.17, bf16[256,16,128]{2,1,0:T(8,128)(2,1)S(1)} %collective-permute-done.1.other_ref, f32[8,128]{1,0:T(8,128)} %constant.17.clone.taper_in, ...), custom_call_target="tpu_custom_call" | custom-call | tf_op jit(solution)/shard_map/grid_tile/pallas_call | solution.py:419
  66.5 20.2 %all_to_all.15.in_ref = bf16[16,128,128]{2,1,0:T(8,128)(2,1)S(1)} all-to-all(bf16[16,128,128]{2,1,0:T(8,128)(2,1)S(1)} %grid_tile.1), channel_id=1, replica_groups=mesh['z'=8,'core'=2,'xh'=2,'xl'=2,'yh'=4,'yl'=2] {'z','core'}, dimensions={0} | all-to-all | bytes 1048576 | tf_op jit(solution)/shard_map/all_to_all | solution.py:456
  86.7 0.8 band_sum.1
Async XLA Ops:
  2.2 37.0 %all-to-all-start = ((bf16[32,24,256]{2,1,0:T(8,128)(2,1)}), bf16[32,24,256]{2,1,0:T(8,128)(2,1)S(1)}, u32[]{:S(2)}, u32[]{:S(2)}) async-start(bf16[32,24,256]{2,1,0:T(8,128)(2,1)} %get-tuple-element.11), calls=%async_computation | async-start | bytes 786432 | tf_op jit(solution)/shard_map/all_to_all | solution.py:448
  39.2 18.3 %all-to-all-start.1 = ((bf16[4,8,8,16,128]{4,3,2,1,0:T(8,128)(2,1)}), bf16[4,8,8,16,128]{4,3,2,1,0:T(8,128)(2,1)S(1)}, u32[]{:S(2)}, u32[]{:S(2)}) async-start(bf16[4,8,8,16,128]{4,3,2,1,0:T(8,128)(2,1)} %collect.1), calls=%async_computation.1 | async-start | bytes 2097152 | tf_op jit(solution)/shard_map/all_to_all | solution.py:450
  42.9 3.7 %collective-permute-start = (bf16[32,24,256]{2,1,0:T(8,128)(2,1)S(1)}, bf16[32,24,256]{2,1,0:T(8,128)(2,1)S(1)}, u32[]{:S(2)}, u32[]{:S(2)}) collective-permute-start(bf16[32,24,256]{2,1,0:T(8,128)(2,1)S(1)} %all-to-all-done), channel_id=1, source_target_pairs={{0,32},{32,0},{1,33},{33,1},{2,34},{34,2},{3,35},{35,3},{4,36},{36... | collective-permute-start | bytes 1179656 | tf_op jit(solution)/shard_map/ppermute | solution.py:451
  56.9 0.6 copy-start
  57.5 4.5 %collective-permute-start.1 = (bf16[256,16,128]{2,1,0:T(8,128)(2,1)S(1)}, bf16[256,16,128]{2,1,0:T(8,128)(2,1)S(1)}, u32[]{:S(2)}, u32[]{:S(2)}) collective-permute-start(bf16[256,16,128]{2,1,0:T(8,128)(2,1)S(1)} %bitcast.16), channel_id=1, source_target_pairs={{0,32},{32,0},{1,33},{33,1},{2,34},{34,2},{3,35},{35,3},{4,36},{36... | collective-permute-start | bytes 3145736 | tf_op jit(solution)/shard_map/ppermute | solution.py:454

commit v5 on v4

--- a/solution.py
+++ b/solution.py
@@ -107,7 +107,26 @@
         (uv_in, uv_ref), (weight_in, weight_ref), (vis_in, vis_ref), (screen_in.at[pl.ds(8 * (2 * lax.axis_index("xl") + lax.axis_index("yl")), 8)], screen_ref),
     )
     copies = fetch(pairs, sem)
-    for copy in copies[:4]:
+
+    def clear(i, c):
+        src_ref[2 * i] = -1
+        src_ref[2 * i + 1] = -1
+        count_ref[i] = 0
+        return c
+
+    lax.fori_loop(0, PEERS, clear, 0, unroll=8)
+
+    copies[0].wait()
+
+    def assign(s, c):
+        t = tile_ref[0, s]
+        before = count_ref[t]
+        src_ref[2 * t + before] = s
+        count_ref[t] = before + 1
+        return c
+
+    lax.fori_loop(0, 32, assign, 0, unroll=4)
+    for copy in copies[1:4]:
         copy.wait()
     uv = uv_ref[...]
     hi = uv.astype(BF16)
@@ -126,22 +145,6 @@
         preferred_element_type=F32,
     )
 
-    def clear(i, c):
-        src_ref[2 * i] = -1
-        src_ref[2 * i + 1] = -1
-        count_ref[i] = 0
-        return c
-
-    lax.fori_loop(0, PEERS, clear, 0, unroll=8)
-
-    def assign(s, c):
-        t = tile_ref[0, s]
-        before = count_ref[t]
-        src_ref[2 * t + before] = s
-        count_ref[t] = before + 1
-        return c
-
-    lax.fori_loop(0, 32, assign, 0, unroll=4)
     row = lax.broadcasted_iota(jnp.int32, (8, 256), 0)
     for copy in copies[4:6]:
         copy.wait()
@@ -160,7 +163,7 @@
         out_ref[n] = jnp.concatenate(low + high + [meta], axis=0).astype(BF16)
         return c
 
-    lax.fori_loop(0, PEERS, one_peer, 0, unroll=4)
+    lax.fori_loop(0, PEERS, one_peer, 0, unroll=16)
     copies[6].wait()
     wide_ref[...] = screen_ref[...].astype(F32).reshape(128, 128)
     parts = [wide_ref[pl.ds(ri, 64, stride=2), :].reshape(8, 8, 128) for ri in range(2)]
@@ -199,7 +202,10 @@
     ints = lax.dot_general(
         pick.astype(F32).astype(BF16), meta, (((1,), (1,)), ((), ())), preferred_element_type=F32
     )
-    ints_ref[...] = ints.astype(jnp.int32)
+    row = lax.broadcasted_iota(jnp.int32, (512, 128), 0)
+    slot = jnp.where(row & 7 < 2, ((row >> 3) & 31) * 4 + (row >> 8) * 2 + (row & 7), -1)
+    chosen = (slot == lax.broadcasted_iota(jnp.int32, (512, 128), 1)).astype(F32).astype(BF16)
+    ints_ref[...] = jnp.dot(ints.astype(BF16), chosen, preferred_element_type=F32).astype(jnp.int32)
     send = pltpu.make_async_copy(ints_ref, ints_out, sem.at[4])
     send.start()
 
@@ -235,11 +241,11 @@
                 one_slot(block_ref, b * PEERS + n, n, j, 4 * n + 2 * b + j)
         return c
 
-    lax.fori_loop(0, PEERS, one_peer, 0, unroll=4)
+    lax.fori_loop(0, PEERS, one_peer, 0, unroll=8)
     send.wait()
 
 
-GROUP = 64
+GROUP = 128
 
 
 def grid_kernel(
@@ -268,7 +274,7 @@
         return jnp.where(mine, own_ref[where], other_ref[where]).astype(F32)
 
     def place(g, k):
-        return (k // 2 % 2) * 256 + (g * (GROUP // 4) + k // 4) * 8 + k % 2
+        return g * GROUP + k
 
     def one_group(g, c):
         lhs_re, lhs_im = [], []
@@ -397,12 +403,12 @@
         image_kernel,
         out_shape=(
             jax.ShapeDtypeStruct((2 * SLOTS, SUB, 128), F32),
-            jax.ShapeDtypeStruct((8, 512), jnp.int32),
+            jax.ShapeDtypeStruct((8, 2 * SLOTS), jnp.int32),
         ),
         in_specs=[VM, VM] + [HBM] * 4,
         out_specs=(VM, HBM),
         scratch_shapes=[pltpu.VMEM(a.shape, a.dtype) for a in args]
-        + [pltpu.VMEM((8, 512), jnp.int32)]
+        + [pltpu.VMEM((8, 2 * SLOTS), jnp.int32)]
         + [pltpu.VMEM((2 * PEERS, 8, 256), F32)] * 3
         + [pltpu.SemaphoreType.DMA((5,))],
         name="images",

time: 88.1 us -> 86.8 us (0.985)
  Pallas kernels: 18.8 us -> 17.6 us
where the time goes in v5:
time: 86.8 us; the launch traced here: 86.2 us
  blocking collectives  45.6 us (53%)
  starting transfers between devices  18.8 us (22%)
  Pallas kernels  17.6 us (20%)
  waiting for transfers between devices  3.6 us (4%)
    all_gather x1, blocking collectives, on_device(): lax.all_gather(mine, ('z', 'core'), axis=0, tiled=True)  25.4 us
    all_to_all x1, blocking collectives, on_device(): lax.all_to_all(partial, ('z', 'core'), split_axis=0, concat_axis=0, tiled...  20.2 us
    all_to_all x1, starting transfers between devices, on_device(): lax.all_to_all(packed, ('xh', 'xl', 'yh', 'yl'), split_axis=0, concat_axi...  10.5 us
    pallas_call x1, Pallas kernels, images(): call(image_kernel, out_shape=(jax.ShapeDtypeStruct((2 * SLOTS, SUB, 128),...  9.94 us
    all_to_all x1, starting transfers between devices, on_device(): lax.all_to_all(collect(quarter), ('xl', 'yl'), split_axis=0, concat_axis=...  3.68 us
    pallas_call x1, Pallas kernels, grid_tile(): call(grid_kernel, out_shape=jax.ShapeDtypeStruct((16, 128, 128), BF16), i...  3.58 us
    ppermute x1, starting transfers between devices, on_device(): sibling = lax.ppermute(recv, 'core', SWAP)  2.34 us
    ppermute x1, starting transfers between devices, on_device(): other = lax.ppermute(own, 'core', SWAP)  2.27 us
  transfers between devices with their start and end apart: 4, of which 2 were waited for; matrix products, arithmetic and copies ran while one was open for 0% of the time, Pallas kernels for 13%

profile of v5, /device:TPU:1, one launch (start us, length us, event | category | flops | bytes accessed | tf_op | source)
XLA Modules:
  0.0 86.2 jit_solution(17048477835603068728)
XLA Ops:
  0.0 2.1 %pack.1 = (bf16[32,24,256]{2,1,0:T(8,128)(2,1)}, bf16[8,16,128]{2,1,0:T(8,128)(2,1)S(1)}) custom-call(s32[1,32]{1,0:T(1,128)} %bitcast.26, f32[32,8,256]{2,1,0:T(8,128)} %vis_in.1, f32[32,256]{1,0:T(8,128)} %weight_in.1, f32[32,32]{1,0:T(8,128)} %bitcast.22, s32[2,32]{1,0:T(2,128)} %bitcast.23, s32[2,32]{1,0:T(2,128)} %bitcast.24, bf16[32,16,128]{2,1,0:T(8,128)(2,1)} %bitcast.21), custom_call_target="tpu_custom_call" | custom-call | tf_op jit(solution)/shard_map/pack/pallas_call | solution.py:366
  2.2 10.5 %all-to-all-start = ((bf16[32,24,256]{2,1,0:T(8,128)(2,1)}), bf16[32,24,256]{2,1,0:T(8,128)(2,1)S(1)}, u32[]{:S(2)}, u32[]{:S(2)}) async-start(bf16[32,24,256]{2,1,0:T(8,128)(2,1)} %get-tuple-element.11), calls=%async_computation | async-start | bytes 786432 | tf_op jit(solution)/shard_map/all_to_all | solution.py:454
  12.7 25.4 %all_gather.3 = bf16[128,16,128]{2,1,0:T(8,128)(2,1)S(1)} all-gather(bf16[8,16,128]{2,1,0:T(8,128)(2,1)S(1)} %get-tuple-element.13), channel_id=1, replica_groups=mesh['z'=8,'core'=2,'xh'=2,'xl'=2,'yh'=4,'yl'=2] {'z','core'}, dimensions={0}, use_global_device_ids=true | all-gather | bytes 557056 | tf_op jit(solution)/shard_map/all_gather | solution.py:455
  38.1 1.1 %collect.1 = bf16[4,8,8,16,128]{4,3,2,1,0:T(8,128)(2,1)} custom-call(bf16[8,2,8,16,128]{4,3,2,1,0:T(8,128)(2,1)S(1)} %bitcast.18), custom_call_target="tpu_custom_call" | custom-call | tf_op jit(solution)/shard_map/collect/pallas_call | solution.py:389
  39.2 0.0 all-to-all-done
  39.2 3.7 %all-to-all-start.1 = ((bf16[4,8,8,16,128]{4,3,2,1,0:T(8,128)(2,1)}), bf16[4,8,8,16,128]{4,3,2,1,0:T(8,128)(2,1)S(1)}, u32[]{:S(2)}, u32[]{:S(2)}) async-start(bf16[4,8,8,16,128]{4,3,2,1,0:T(8,128)(2,1)} %collect.1), calls=%async_computation.1 | async-start | bytes 2097152 | tf_op jit(solution)/shard_map/all_to_all | solution.py:456
  42.9 2.3 %collective-permute-start = (bf16[32,24,256]{2,1,0:T(8,128)(2,1)S(1)}, bf16[32,24,256]{2,1,0:T(8,128)(2,1)S(1)}, u32[]{:S(2)}, u32[]{:S(2)}) collective-permute-start(bf16[32,24,256]{2,1,0:T(8,128)(2,1)S(1)} %all-to-all-done), channel_id=1, source_target_pairs={{0,32},{32,0},{1,33},{33,1},{2,34},{34,2},{3,35},{35,3},{4,36},{36... | collective-permute-start | bytes 1179656 | tf_op jit(solution)/shard_map/ppermute | solution.py:457
  45.2 1.3 %collective-permute-done = bf16[32,24,256]{2,1,0:T(8,128)(2,1)S(1)} collective-permute-done((bf16[32,24,256]{2,1,0:T(8,128)(2,1)S(1)}, bf16[32,24,256]{2,1,0:T(8,128)(2,1)S(1)}, u32[]{:S(2)}, u32[]{:S(2)}) %collective-permute-start) | collective-permute-done | bytes 393248 | tf_op jit(solution)/shard_map/ppermute | solution.py:457
  46.5 9.9 %images.1 = (f32[128,32,128]{2,1,0:T(8,128)S(1)}, s32[8,128]{1,0:T(8,128)S(1)}) custom-call(bf16[96,8,256]{2,1,0:T(8,128)(2,1)S(1)} %bitcast.19, bf16[96,8,256]{2,1,0:T(8,128)(2,1)S(1)} %bitcast.20, f32[1,16]{1,0:T(1,128)} %bitcast.25, bf16[4,256,256]{2,1,0:T(8,128)(2,1)} %constant.14.clone.spread_in, f32[32,256]{1,0:T(8,128)} %constant.15.clone.xrow_in, ...), custom_call_target="tpu_custom_call" | custom-call | tf_op jit(solution)/shard_map/images/pallas_call | solution.py:402
  56.5 0.0 copy-start
  56.5 0.6 copy-done
  57.1 0.0 all-to-all-done.1
  57.1 2.3 %collective-permute-start.1 = (bf16[256,16,128]{2,1,0:T(8,128)(2,1)S(1)}, bf16[256,16,128]{2,1,0:T(8,128)(2,1)S(1)}, u32[]{:S(2)}, u32[]{:S(2)}) collective-permute-start(bf16[256,16,128]{2,1,0:T(8,128)(2,1)S(1)} %bitcast.16), channel_id=1, source_target_pairs={{0,32},{32,0},{1,33},{33,1},{2,34},{34,2},{3,35},{35,3},{4,36},{36... | collective-permute-start | bytes 3145736 | tf_op jit(solution)/shard_map/ppermute | solution.py:460
  59.3 2.3 %collective-permute-done.1.other_ref = bf16[256,16,128]{2,1,0:T(8,128)(2,1)S(1)} collective-permute-done((bf16[256,16,128]{2,1,0:T(8,128)(2,1)S(1)}, bf16[256,16,128]{2,1,0:T(8,128)(2,1)S(1)}, u32[]{:S(2)}, u32[]{:S(2)}) %collective-permute-start.1) | collective-permute-done | bytes 1048608 | tf_op jit(solution)/shard_map/ppermute | solution.py:460
  61.6 3.6 %grid_tile.1 = bf16[16,128,128]{2,1,0:T(8,128)(2,1)S(1)} custom-call(s32[8,128]{1,0:T(8,128)} %copy-done, f32[128,32,128]{2,1,0:T(8,128)S(1)} %get-tuple-element.15.i_ref, bf16[256,16,128]{2,1,0:T(8,128)(2,1)S(1)} %bitcast.17, bf16[256,16,128]{2,1,0:T(8,128)(2,1)S(1)} %collective-permute-done.1.other_ref, f32[8,128]{1,0:T(8,128)} %constant.17.clone.taper_in, ...), custom_call_target="tpu_custom_call" | custom-call | tf_op jit(solution)/shard_map/grid_tile/pallas_call | solution.py:425
  65.2 20.2 %all_to_all.15.in_ref = bf16[16,128,128]{2,1,0:T(8,128)(2,1)S(1)} all-to-all(bf16[16,128,128]{2,1,0:T(8,128)(2,1)S(1)} %grid_tile.1), channel_id=1, replica_groups=mesh['z'=8,'core'=2,'xh'=2,'xl'=2,'yh'=4,'yl'=2] {'z','core'}, dimensions={0} | all-to-all | bytes 1048576 | tf_op jit(solution)/shard_map/all_to_all | solution.py:462
  85.4 0.8 band_sum.1
Async XLA Ops:
  2.2 37.0 %all-to-all-start = ((bf16[32,24,256]{2,1,0:T(8,128)(2,1)}), bf16[32,24,256]{2,1,0:T(8,128)(2,1)S(1)}, u32[]{:S(2)}, u32[]{:S(2)}) async-start(bf16[32,24,256]{2,1,0:T(8,128)(2,1)} %get-tuple-element.11), calls=%async_computation | async-start | bytes 786432 | tf_op jit(solution)/shard_map/all_to_all | solution.py:454
  39.2 17.9 %all-to-all-start.1 = ((bf16[4,8,8,16,128]{4,3,2,1,0:T(8,128)(2,1)}), bf16[4,8,8,16,128]{4,3,2,1,0:T(8,128)(2,1)S(1)}, u32[]{:S(2)}, u32[]{:S(2)}) async-start(bf16[4,8,8,16,128]{4,3,2,1,0:T(8,128)(2,1)} %collect.1), calls=%async_computation.1 | async-start | bytes 2097152 | tf_op jit(solution)/shard_map/all_to_all | solution.py:456
  42.9 3.7 %collective-permute-start = (bf16[32,24,256]{2,1,0:T(8,128)(2,1)S(1)}, bf16[32,24,256]{2,1,0:T(8,128)(2,1)S(1)}, u32[]{:S(2)}, u32[]{:S(2)}) collective-permute-start(bf16[32,24,256]{2,1,0:T(8,128)(2,1)S(1)} %all-to-all-done), channel_id=1, source_target_pairs={{0,32},{32,0},{1,33},{33,1},{2,34},{34,2},{3,35},{35,3},{4,36},{36... | collective-permute-start | bytes 1179656 | tf_op jit(solution)/shard_map/ppermute | solution.py:457
  56.5 0.6 copy-start
  57.1 4.5 %collective-permute-start.1 = (bf16[256,16,128]{2,1,0:T(8,128)(2,1)S(1)}, bf16[256,16,128]{2,1,0:T(8,128)(2,1)S(1)}, u32[]{:S(2)}, u32[]{:S(2)}) collective-permute-start(bf16[256,16,128]{2,1,0:T(8,128)(2,1)S(1)} %bitcast.16), channel_id=1, source_target_pairs={{0,32},{32,0},{1,33},{33,1},{2,34},{34,2},{3,35},{35,3},{4,36},{36... | collective-permute-start | bytes 3145736 | tf_op jit(solution)/shard_map/ppermute | solution.py:460

commit v6 on v5

--- a/solution.py
+++ b/solution.py
@@ -326,7 +326,7 @@
     for band in range(16):
         for a in range(8):
             piece = acc_ref[a, 2 * band : 2 * band + 2].reshape(16, 128)
-            out_ref[band, a * 16 : a * 16 + 16, :] = piece.astype(BF16)
+            out_ref[(band % 2) * 8 + band // 2, a * 16 : a * 16 + 16, :] = piece.astype(BF16)
 
 
 def sum_kernel(in_ref, out_ref):
@@ -337,9 +337,9 @@
             parts = []
             for a in range(4):
                 at = (h * 4 + a) * 16
-                total = in_ref[core, at : at + 16, :].astype(F32)
+                total = in_ref[8 * core, at : at + 16, :].astype(F32)
                 for z in range(1, 8):
-                    total = total + in_ref[2 * z + core, at : at + 16, :].astype(F32)
+                    total = total + in_ref[8 * core + z, at : at + 16, :].astype(F32)
                 parts.append(total)
             for g in range(4):
                 row = jnp.zeros((16, 128), F32)
@@ -459,7 +459,7 @@
     own, image = lax.optimization_barrier((own, image))
     other = lax.ppermute(own, "core", SWAP)
     partial = grid_tile(ints, image, own, other)
-    arrived = lax.all_to_all(partial, ("z", "core"), split_axis=0, concat_axis=0, tiled=True)
+    arrived = lax.all_to_all(partial, ("core", "z"), split_axis=0, concat_axis=0, tiled=True)
     return band_sum(arrived)
 
 

time: 86.8 us -> 84.9 us (0.978)
  blocking collectives: 45.6 us -> 43.1 us
    all_to_all x1, blocking collectives: 20.2 us -> 17.7 us  [on_device(): lax.all_to_all(partial, ('core', 'z'), split_axis=0, concat_axis=0, tiled...]
where the time goes in v6:
time: 84.9 us; the launch traced here: 83.7 us
  blocking collectives  43.1 us (51%)
  starting transfers between devices  18.8 us (22%)
  Pallas kernels  17.6 us (21%)
  waiting for transfers between devices  3.6 us (4%)
    all_gather x1, blocking collectives, on_device(): lax.all_gather(mine, ('z', 'core'), axis=0, tiled=True)  25.4 us
    all_to_all x1, blocking collectives, on_device(): lax.all_to_all(partial, ('core', 'z'), split_axis=0, concat_axis=0, tiled...  17.7 us
    all_to_all x1, starting transfers between devices, on_device(): lax.all_to_all(packed, ('xh', 'xl', 'yh', 'yl'), split_axis=0, concat_axi...  10.5 us
    pallas_call x1, Pallas kernels, images(): call(image_kernel, out_shape=(jax.ShapeDtypeStruct((2 * SLOTS, SUB, 128),...  9.94 us
    all_to_all x1, starting transfers between devices, on_device(): lax.all_to_all(collect(quarter), ('xl', 'yl'), split_axis=0, concat_axis=...  3.68 us
    pallas_call x1, Pallas kernels, grid_tile(): call(grid_kernel, out_shape=jax.ShapeDtypeStruct((16, 128, 128), BF16), i...  3.58 us
    ppermute x1, starting transfers between devices, on_device(): sibling = lax.ppermute(recv, 'core', SWAP)  2.34 us
    ppermute x1, starting transfers between devices, on_device(): other = lax.ppermute(own, 'core', SWAP)  2.27 us
  transfers between devices with their start and end apart: 4, of which 2 were waited for; matrix products, arithmetic and copies ran while one was open for 0% of the time, Pallas kernels for 13%

profile of v6, /device:TPU:1, one launch (start us, length us, event | category | flops | bytes accessed | tf_op | source)
XLA Modules:
  0.0 83.7 jit_solution(14593582992150442742)
XLA Ops:
  0.0 2.1 %pack.1 = (bf16[32,24,256]{2,1,0:T(8,128)(2,1)}, bf16[8,16,128]{2,1,0:T(8,128)(2,1)S(1)}) custom-call(s32[1,32]{1,0:T(1,128)} %bitcast.26, f32[32,8,256]{2,1,0:T(8,128)} %vis_in.1, f32[32,256]{1,0:T(8,128)} %weight_in.1, f32[32,32]{1,0:T(8,128)} %bitcast.22, s32[2,32]{1,0:T(2,128)} %bitcast.23, s32[2,32]{1,0:T(2,128)} %bitcast.24, bf16[32,16,128]{2,1,0:T(8,128)(2,1)} %bitcast.21), custom_call_target="tpu_custom_call" | custom-call | tf_op jit(solution)/shard_map/pack/pallas_call | solution.py:366
  2.2 10.5 %all-to-all-start = ((bf16[32,24,256]{2,1,0:T(8,128)(2,1)}), bf16[32,24,256]{2,1,0:T(8,128)(2,1)S(1)}, u32[]{:S(2)}, u32[]{:S(2)}) async-start(bf16[32,24,256]{2,1,0:T(8,128)(2,1)} %get-tuple-element.11), calls=%async_computation | async-start | bytes 786432 | tf_op jit(solution)/shard_map/all_to_all | solution.py:454
  12.7 25.4 %all_gather.3 = bf16[128,16,128]{2,1,0:T(8,128)(2,1)S(1)} all-gather(bf16[8,16,128]{2,1,0:T(8,128)(2,1)S(1)} %get-tuple-element.13), channel_id=1, replica_groups=mesh['z'=8,'core'=2,'xh'=2,'xl'=2,'yh'=4,'yl'=2] {'z','core'}, dimensions={0}, use_global_device_ids=true | all-gather | bytes 557056 | tf_op jit(solution)/shard_map/all_gather | solution.py:455
  38.1 1.1 %collect.1 = bf16[4,8,8,16,128]{4,3,2,1,0:T(8,128)(2,1)} custom-call(bf16[8,2,8,16,128]{4,3,2,1,0:T(8,128)(2,1)S(1)} %bitcast.18), custom_call_target="tpu_custom_call" | custom-call | tf_op jit(solution)/shard_map/collect/pallas_call | solution.py:389
  39.2 0.0 all-to-all-done
  39.2 3.7 %all-to-all-start.1 = ((bf16[4,8,8,16,128]{4,3,2,1,0:T(8,128)(2,1)}), bf16[4,8,8,16,128]{4,3,2,1,0:T(8,128)(2,1)S(1)}, u32[]{:S(2)}, u32[]{:S(2)}) async-start(bf16[4,8,8,16,128]{4,3,2,1,0:T(8,128)(2,1)} %collect.1), calls=%async_computation.1 | async-start | bytes 2097152 | tf_op jit(solution)/shard_map/all_to_all | solution.py:456
  42.9 2.3 %collective-permute-start = (bf16[32,24,256]{2,1,0:T(8,128)(2,1)S(1)}, bf16[32,24,256]{2,1,0:T(8,128)(2,1)S(1)}, u32[]{:S(2)}, u32[]{:S(2)}) collective-permute-start(bf16[32,24,256]{2,1,0:T(8,128)(2,1)S(1)} %all-to-all-done), channel_id=1, source_target_pairs={{0,32},{32,0},{1,33},{33,1},{2,34},{34,2},{3,35},{35,3},{4,36},{36... | collective-permute-start | bytes 1179656 | tf_op jit(solution)/shard_map/ppermute | solution.py:457
  45.2 1.3 %collective-permute-done = bf16[32,24,256]{2,1,0:T(8,128)(2,1)S(1)} collective-permute-done((bf16[32,24,256]{2,1,0:T(8,128)(2,1)S(1)}, bf16[32,24,256]{2,1,0:T(8,128)(2,1)S(1)}, u32[]{:S(2)}, u32[]{:S(2)}) %collective-permute-start) | collective-permute-done | bytes 393248 | tf_op jit(solution)/shard_map/ppermute | solution.py:457
  46.5 9.9 %images.1 = (f32[128,32,128]{2,1,0:T(8,128)S(1)}, s32[8,128]{1,0:T(8,128)S(1)}) custom-call(bf16[96,8,256]{2,1,0:T(8,128)(2,1)S(1)} %bitcast.19, bf16[96,8,256]{2,1,0:T(8,128)(2,1)S(1)} %bitcast.20, f32[1,16]{1,0:T(1,128)} %bitcast.25, bf16[4,256,256]{2,1,0:T(8,128)(2,1)} %constant.14.clone.spread_in, f32[32,256]{1,0:T(8,128)} %constant.15.clone.xrow_in, ...), custom_call_target="tpu_custom_call" | custom-call | tf_op jit(solution)/shard_map/images/pallas_call | solution.py:402
  56.5 0.0 copy-start
  56.5 0.6 copy-done
  57.1 0.0 all-to-all-done.1
  57.1 2.3 %collective-permute-start.1 = (bf16[256,16,128]{2,1,0:T(8,128)(2,1)S(1)}, bf16[256,16,128]{2,1,0:T(8,128)(2,1)S(1)}, u32[]{:S(2)}, u32[]{:S(2)}) collective-permute-start(bf16[256,16,128]{2,1,0:T(8,128)(2,1)S(1)} %bitcast.16), channel_id=1, source_target_pairs={{0,32},{32,0},{1,33},{33,1},{2,34},{34,2},{3,35},{35,3},{4,36},{36... | collective-permute-start | bytes 3145736 | tf_op jit(solution)/shard_map/ppermute | solution.py:460
  59.3 2.3 %collective-permute-done.1.other_ref = bf16[256,16,128]{2,1,0:T(8,128)(2,1)S(1)} collective-permute-done((bf16[256,16,128]{2,1,0:T(8,128)(2,1)S(1)}, bf16[256,16,128]{2,1,0:T(8,128)(2,1)S(1)}, u32[]{:S(2)}, u32[]{:S(2)}) %collective-permute-start.1) | collective-permute-done | bytes 1048608 | tf_op jit(solution)/shard_map/ppermute | solution.py:460
  61.6 3.6 %grid_tile.1 = bf16[16,128,128]{2,1,0:T(8,128)(2,1)S(1)} custom-call(s32[8,128]{1,0:T(8,128)} %copy-done, f32[128,32,128]{2,1,0:T(8,128)S(1)} %get-tuple-element.15.i_ref, bf16[256,16,128]{2,1,0:T(8,128)(2,1)S(1)} %bitcast.17, bf16[256,16,128]{2,1,0:T(8,128)(2,1)S(1)} %collective-permute-done.1.other_ref, f32[8,128]{1,0:T(8,128)} %constant.17.clone.taper_in, ...), custom_call_target="tpu_custom_call" | custom-call | tf_op jit(solution)/shard_map/grid_tile/pallas_call | solution.py:425
  65.2 17.7 %all_to_all.15.in_ref = bf16[16,128,128]{2,1,0:T(8,128)(2,1)S(1)} all-to-all(bf16[16,128,128]{2,1,0:T(8,128)(2,1)S(1)} %grid_tile.1), channel_id=1, replica_groups=mesh['z'=8,'core'=2,'xh'=2,'xl'=2,'yh'=4,'yl'=2] {'core','z'}, dimensions={0} | all-to-all | bytes 1048576 | tf_op jit(solution)/shard_map/all_to_all | solution.py:462
  82.9 0.8 band_sum.1
Async XLA Ops:
  2.2 37.0 %all-to-all-start = ((bf16[32,24,256]{2,1,0:T(8,128)(2,1)}), bf16[32,24,256]{2,1,0:T(8,128)(2,1)S(1)}, u32[]{:S(2)}, u32[]{:S(2)}) async-start(bf16[32,24,256]{2,1,0:T(8,128)(2,1)} %get-tuple-element.11), calls=%async_computation | async-start | bytes 786432 | tf_op jit(solution)/shard_map/all_to_all | solution.py:454
  39.2 17.9 %all-to-all-start.1 = ((bf16[4,8,8,16,128]{4,3,2,1,0:T(8,128)(2,1)}), bf16[4,8,8,16,128]{4,3,2,1,0:T(8,128)(2,1)S(1)}, u32[]{:S(2)}, u32[]{:S(2)}) async-start(bf16[4,8,8,16,128]{4,3,2,1,0:T(8,128)(2,1)} %collect.1), calls=%async_computation.1 | async-start | bytes 2097152 | tf_op jit(solution)/shard_map/all_to_all | solution.py:456
  42.9 3.7 %collective-permute-start = (bf16[32,24,256]{2,1,0:T(8,128)(2,1)S(1)}, bf16[32,24,256]{2,1,0:T(8,128)(2,1)S(1)}, u32[]{:S(2)}, u32[]{:S(2)}) collective-permute-start(bf16[32,24,256]{2,1,0:T(8,128)(2,1)S(1)} %all-to-all-done), channel_id=1, source_target_pairs={{0,32},{32,0},{1,33},{33,1},{2,34},{34,2},{3,35},{35,3},{4,36},{36... | collective-permute-start | bytes 1179656 | tf_op jit(solution)/shard_map/ppermute | solution.py:457
  56.5 0.6 copy-start
  57.1 4.5 %collective-permute-start.1 = (bf16[256,16,128]{2,1,0:T(8,128)(2,1)S(1)}, bf16[256,16,128]{2,1,0:T(8,128)(2,1)S(1)}, u32[]{:S(2)}, u32[]{:S(2)}) collective-permute-start(bf16[256,16,128]{2,1,0:T(8,128)(2,1)S(1)} %bitcast.16), channel_id=1, source_target_pairs={{0,32},{32,0},{1,33},{33,1},{2,34},{34,2},{3,35},{35,3},{4,36},{36... | collective-permute-start | bytes 3145736 | tf_op jit(solution)/shard_map/ppermute | solution.py:460

commit v7 on v6

--- a/solution.py
+++ b/solution.py
@@ -104,7 +104,7 @@
 ):
     pairs = (
         (tile_in, tile_ref), (station_in, station_ref), (offset_in, offset_ref),
-        (uv_in, uv_ref), (weight_in, weight_ref), (vis_in, vis_ref), (screen_in.at[pl.ds(8 * (2 * lax.axis_index("xl") + lax.axis_index("yl")), 8)], screen_ref),
+        (uv_in, uv_ref), (weight_in, weight_ref), (vis_in, vis_ref), (screen_in.at[pl.ds(8 * (2 * lax.axis_index("yl") + lax.axis_index("xl")), 8)], screen_ref),
     )
     copies = fetch(pairs, sem)
 
@@ -453,7 +453,7 @@
     packed, mine = pack(tile_ids.T, visibilities, weights, uv, stations.T, offsets.T, pairs)
     recv = lax.all_to_all(packed, ("xh", "xl", "yh", "yl"), split_axis=0, concat_axis=0, tiled=True)
     quarter = lax.all_gather(mine, ("z", "core"), axis=0, tiled=True).reshape(8, 2, 8, 16, 128)
-    own = lax.all_to_all(collect(quarter), ("xl", "yl"), split_axis=0, concat_axis=0, tiled=True).reshape(256, 16, 128)
+    own = lax.all_to_all(collect(quarter), ("yl", "xl"), split_axis=0, concat_axis=0, tiled=True).reshape(256, 16, 128)
     sibling = lax.ppermute(recv, "core", SWAP)
     image, ints = images(recv.reshape(96, 8, 256), sibling.reshape(96, 8, 256), freq_ratio[None, :])
     own, image = lax.optimization_barrier((own, image))

time: 84.9 us -> 84.9 us (level)
  no operation moved by 1% of the time
where the time goes in v7:
time: 84.9 us; the launch traced here: 83.7 us
  blocking collectives  43.1 us (51%)
  starting transfers between devices  18.8 us (22%)
  Pallas kernels  17.6 us (21%)
  waiting for transfers between devices  3.6 us (4%)
    all_gather x1, blocking collectives, on_device(): lax.all_gather(mine, ('z', 'core'), axis=0, tiled=True)  25.4 us
    all_to_all x1, blocking collectives, on_device(): lax.all_to_all(partial, ('core', 'z'), split_axis=0, concat_axis=0, tiled...  17.7 us
    all_to_all x1, starting transfers between devices, on_device(): lax.all_to_all(packed, ('xh', 'xl', 'yh', 'yl'), split_axis=0, concat_axi...  10.5 us
    pallas_call x1, Pallas kernels, images(): call(image_kernel, out_shape=(jax.ShapeDtypeStruct((2 * SLOTS, SUB, 128),...  9.94 us
    all_to_all x1, starting transfers between devices, on_device(): lax.all_to_all(collect(quarter), ('yl', 'xl'), split_axis=0, concat_axis=...  3.68 us
    pallas_call x1, Pallas kernels, grid_tile(): call(grid_kernel, out_shape=jax.ShapeDtypeStruct((16, 128, 128), BF16), i...  3.58 us
    ppermute x1, starting transfers between devices, on_device(): sibling = lax.ppermute(recv, 'core', SWAP)  2.34 us
    ppermute x1, starting transfers between devices, on_device(): other = lax.ppermute(own, 'core', SWAP)  2.27 us
  transfers between devices with their start and end apart: 4, of which 2 were waited for; matrix products, arithmetic and copies ran while one was open for 0% of the time, Pallas kernels for 13%

profile of v7, /device:TPU:1, one launch (start us, length us, event | category | flops | bytes accessed | tf_op | source)
XLA Modules:
  0.0 83.7 jit_solution(14585697653359624137)
XLA Ops:
  0.0 2.1 %pack.1 = (bf16[32,24,256]{2,1,0:T(8,128)(2,1)}, bf16[8,16,128]{2,1,0:T(8,128)(2,1)S(1)}) custom-call(s32[1,32]{1,0:T(1,128)} %bitcast.26, f32[32,8,256]{2,1,0:T(8,128)} %vis_in.1, f32[32,256]{1,0:T(8,128)} %weight_in.1, f32[32,32]{1,0:T(8,128)} %bitcast.22, s32[2,32]{1,0:T(2,128)} %bitcast.23, s32[2,32]{1,0:T(2,128)} %bitcast.24, bf16[32,16,128]{2,1,0:T(8,128)(2,1)} %bitcast.21), custom_call_target="tpu_custom_call" | custom-call | tf_op jit(solution)/shard_map/pack/pallas_call | solution.py:366
  2.2 10.5 %all-to-all-start = ((bf16[32,24,256]{2,1,0:T(8,128)(2,1)}), bf16[32,24,256]{2,1,0:T(8,128)(2,1)S(1)}, u32[]{:S(2)}, u32[]{:S(2)}) async-start(bf16[32,24,256]{2,1,0:T(8,128)(2,1)} %get-tuple-element.11), calls=%async_computation | async-start | bytes 786432 | tf_op jit(solution)/shard_map/all_to_all | solution.py:454
  12.7 25.4 %all_gather.3 = bf16[128,16,128]{2,1,0:T(8,128)(2,1)S(1)} all-gather(bf16[8,16,128]{2,1,0:T(8,128)(2,1)S(1)} %get-tuple-element.13), channel_id=1, replica_groups=mesh['z'=8,'core'=2,'xh'=2,'xl'=2,'yh'=4,'yl'=2] {'z','core'}, dimensions={0}, use_global_device_ids=true | all-gather | bytes 557056 | tf_op jit(solution)/shard_map/all_gather | solution.py:455
  38.1 1.1 %collect.1 = bf16[4,8,8,16,128]{4,3,2,1,0:T(8,128)(2,1)} custom-call(bf16[8,2,8,16,128]{4,3,2,1,0:T(8,128)(2,1)S(1)} %bitcast.18), custom_call_target="tpu_custom_call" | custom-call | tf_op jit(solution)/shard_map/collect/pallas_call | solution.py:389
  39.2 0.0 all-to-all-done
  39.2 3.7 %all-to-all-start.1 = ((bf16[4,8,8,16,128]{4,3,2,1,0:T(8,128)(2,1)}), bf16[4,8,8,16,128]{4,3,2,1,0:T(8,128)(2,1)S(1)}, u32[]{:S(2)}, u32[]{:S(2)}) async-start(bf16[4,8,8,16,128]{4,3,2,1,0:T(8,128)(2,1)} %collect.1), calls=%async_computation.1 | async-start | bytes 2097152 | tf_op jit(solution)/shard_map/all_to_all | solution.py:456
  42.9 2.3 %collective-permute-start = (bf16[32,24,256]{2,1,0:T(8,128)(2,1)S(1)}, bf16[32,24,256]{2,1,0:T(8,128)(2,1)S(1)}, u32[]{:S(2)}, u32[]{:S(2)}) collective-permute-start(bf16[32,24,256]{2,1,0:T(8,128)(2,1)S(1)} %all-to-all-done), channel_id=1, source_target_pairs={{0,32},{32,0},{1,33},{33,1},{2,34},{34,2},{3,35},{35,3},{4,36},{36... | collective-permute-start | bytes 1179656 | tf_op jit(solution)/shard_map/ppermute | solution.py:457
  45.2 1.3 %collective-permute-done = bf16[32,24,256]{2,1,0:T(8,128)(2,1)S(1)} collective-permute-done((bf16[32,24,256]{2,1,0:T(8,128)(2,1)S(1)}, bf16[32,24,256]{2,1,0:T(8,128)(2,1)S(1)}, u32[]{:S(2)}, u32[]{:S(2)}) %collective-permute-start) | collective-permute-done | bytes 393248 | tf_op jit(solution)/shard_map/ppermute | solution.py:457
  46.5 9.9 %images.1 = (f32[128,32,128]{2,1,0:T(8,128)S(1)}, s32[8,128]{1,0:T(8,128)S(1)}) custom-call(bf16[96,8,256]{2,1,0:T(8,128)(2,1)S(1)} %bitcast.19, bf16[96,8,256]{2,1,0:T(8,128)(2,1)S(1)} %bitcast.20, f32[1,16]{1,0:T(1,128)} %bitcast.25, bf16[4,256,256]{2,1,0:T(8,128)(2,1)} %constant.14.clone.spread_in, f32[32,256]{1,0:T(8,128)} %constant.15.clone.xrow_in, ...), custom_call_target="tpu_custom_call" | custom-call | tf_op jit(solution)/shard_map/images/pallas_call | solution.py:402
  56.5 0.0 copy-start
  56.5 0.6 copy-done
  57.1 0.0 all-to-all-done.1
  57.1 2.3 %collective-permute-start.1 = (bf16[256,16,128]{2,1,0:T(8,128)(2,1)S(1)}, bf16[256,16,128]{2,1,0:T(8,128)(2,1)S(1)}, u32[]{:S(2)}, u32[]{:S(2)}) collective-permute-start(bf16[256,16,128]{2,1,0:T(8,128)(2,1)S(1)} %bitcast.16), channel_id=1, source_target_pairs={{0,32},{32,0},{1,33},{33,1},{2,34},{34,2},{3,35},{35,3},{4,36},{36... | collective-permute-start | bytes 3145736 | tf_op jit(solution)/shard_map/ppermute | solution.py:460
  59.4 2.3 %collective-permute-done.1.other_ref = bf16[256,16,128]{2,1,0:T(8,128)(2,1)S(1)} collective-permute-done((bf16[256,16,128]{2,1,0:T(8,128)(2,1)S(1)}, bf16[256,16,128]{2,1,0:T(8,128)(2,1)S(1)}, u32[]{:S(2)}, u32[]{:S(2)}) %collective-permute-start.1) | collective-permute-done | bytes 1048608 | tf_op jit(solution)/shard_map/ppermute | solution.py:460
  61.6 3.6 %grid_tile.1 = bf16[16,128,128]{2,1,0:T(8,128)(2,1)S(1)} custom-call(s32[8,128]{1,0:T(8,128)} %copy-done, f32[128,32,128]{2,1,0:T(8,128)S(1)} %get-tuple-element.15.i_ref, bf16[256,16,128]{2,1,0:T(8,128)(2,1)S(1)} %bitcast.17, bf16[256,16,128]{2,1,0:T(8,128)(2,1)S(1)} %collective-permute-done.1.other_ref, f32[8,128]{1,0:T(8,128)} %constant.17.clone.taper_in, ...), custom_call_target="tpu_custom_call" | custom-call | tf_op jit(solution)/shard_map/grid_tile/pallas_call | solution.py:425
  65.2 17.7 %all_to_all.15.in_ref = bf16[16,128,128]{2,1,0:T(8,128)(2,1)S(1)} all-to-all(bf16[16,128,128]{2,1,0:T(8,128)(2,1)S(1)} %grid_tile.1), channel_id=1, replica_groups=mesh['z'=8,'core'=2,'xh'=2,'xl'=2,'yh'=4,'yl'=2] {'core','z'}, dimensions={0} | all-to-all | bytes 1048576 | tf_op jit(solution)/shard_map/all_to_all | solution.py:462
  82.9 0.8 band_sum.1
Async XLA Ops:
  2.2 37.0 %all-to-all-start = ((bf16[32,24,256]{2,1,0:T(8,128)(2,1)}), bf16[32,24,256]{2,1,0:T(8,128)(2,1)S(1)}, u32[]{:S(2)}, u32[]{:S(2)}) async-start(bf16[32,24,256]{2,1,0:T(8,128)(2,1)} %get-tuple-element.11), calls=%async_computation | async-start | bytes 786432 | tf_op jit(solution)/shard_map/all_to_all | solution.py:454
  39.2 17.9 %all-to-all-start.1 = ((bf16[4,8,8,16,128]{4,3,2,1,0:T(8,128)(2,1)}), bf16[4,8,8,16,128]{4,3,2,1,0:T(8,128)(2,1)S(1)}, u32[]{:S(2)}, u32[]{:S(2)}) async-start(bf16[4,8,8,16,128]{4,3,2,1,0:T(8,128)(2,1)} %collect.1), calls=%async_computation.1 | async-start | bytes 2097152 | tf_op jit(solution)/shard_map/all_to_all | solution.py:456
  42.9 3.7 %collective-permute-start = (bf16[32,24,256]{2,1,0:T(8,128)(2,1)S(1)}, bf16[32,24,256]{2,1,0:T(8,128)(2,1)S(1)}, u32[]{:S(2)}, u32[]{:S(2)}) collective-permute-start(bf16[32,24,256]{2,1,0:T(8,128)(2,1)S(1)} %all-to-all-done), channel_id=1, source_target_pairs={{0,32},{32,0},{1,33},{33,1},{2,34},{34,2},{3,35},{35,3},{4,36},{36... | collective-permute-start | bytes 1179656 | tf_op jit(solution)/shard_map/ppermute | solution.py:457
  56.5 0.6 copy-start
  57.1 4.5 %collective-permute-start.1 = (bf16[256,16,128]{2,1,0:T(8,128)(2,1)S(1)}, bf16[256,16,128]{2,1,0:T(8,128)(2,1)S(1)}, u32[]{:S(2)}, u32[]{:S(2)}) collective-permute-start(bf16[256,16,128]{2,1,0:T(8,128)(2,1)S(1)} %bitcast.16), channel_id=1, source_target_pairs={{0,32},{32,0},{1,33},{33,1},{2,34},{34,2},{3,35},{35,3},{4,36},{36... | collective-permute-start | bytes 3145736 | tf_op jit(solution)/shard_map/ppermute | solution.py:460
